TPU v7x, 32 devices: a whole 2x2x4 slice. The times are simulated.
32 devices in a mesh: slab: 4 (over y, core), inner: 8 (over z, x).
Axes of the slice: x: 2, y: 2, z: 4, core: 2. Of those that a mesh axis runs over, the one named last changes fastest.
Arguments:
- x_in: bfloat16 [8192, 16384], P(('slab', 'inner')), may hold values from -6 to 6
- bc_in: bfloat16 [8192, 4096], P(('slab', 'inner')), may hold values from -6 to 6
- dt_raw: bfloat16 [8192, 256], P(('slab', 'inner')), may hold values from -6.7 to -4.3
- dt_bias: float32 [256], replicated, may hold values from -0.5 to 0.5
- a_log: float32 [256], replicated, may hold values from -8 to 0, as said below
- d_skip: float32 [256], replicated, may hold values from 0.5 to 1.5
- conv_x_weight: float32 [4, 16384], replicated, may hold values from -3 to 3
- conv_x_bias: float32 [16384], replicated, may hold values from -3 to 3
- conv_bc_weight: float32 [4, 4096], replicated, may hold values from -3 to 3
- conv_bc_bias: float32 [4096], replicated, may hold values from -3 to 3
Outputs:
- y_out: bfloat16 [8192, 16384], P('slab', 'inner')
Inputs may be any that keep to these rules, and one draw needn't show every extreme that they name: `a_log`: per-head logarithm of the decay rate.
All inputs are finite; a program needn't handle non-finite values.
Results may differ from a plain program's by a relative error of at most 0.0034.
Values may be sent and summed in bfloat16 or wider, within the bound.
No kernel may reach another device: no remote copies, remote signals or barrier semaphores. Data moves between devices by JAX's collectives and lax.ppermute only.
A program may use at most 256 MiB of HBM per device.

v0:
```python
import jax
import jax.numpy as jnp
from jax import lax
from jax.experimental import pallas as pl
from jax.experimental.pallas import tpu as pltpu
from jax.sharding import PartitionSpec as P


HEADS = 256
HEADDIM = 64
STATE = 256
GROUPS = 8
CONV = 4
LANES = 128
EDGE_ROWS = 8
SENT_ROWS = 4
SEG = 16


F32 = jnp.float32
BF16 = jnp.bfloat16
ANY = pl.BlockSpec(memory_space=pl.ANY)


def whole(shape):
    return pl.BlockSpec(shape, lambda *_: (0,) * len(shape))


def params():
    return pltpu.CompilerParams(vmem_limit_bytes=63 << 20)


def cost(flops, moved):
    return pl.CostEstimate(flops=flops, bytes_accessed=moved, transcendentals=0)


def chunk_widths(channels):
    return [channels // 4] * 4


def rows_ahead(edge_ref):
    e = edge_ref[...].astype(F32)
    return jnp.concatenate([jnp.zeros((EDGE_ROWS - SENT_ROWS, e.shape[1]), F32), e], axis=0)


def silu(x):
    half = 0.5 * x
    return half + half * jnp.tanh(half)


def conv_rows(carry, rows, weight, bias):
    ext = jnp.concatenate([carry, rows], axis=0)
    acc = bias + weight[CONV - 1 : CONV] * rows
    for back in range(1, CONV):
        shifted = pltpu.roll(ext, back, 0)[EDGE_ROWS:]
        acc = acc + weight[CONV - 1 - back : CONV - back] * shifted
    return silu(acc).astype(BF16)


def spread(per_head, heads_dev, first, width):
    return jnp.dot(per_head, pick(heads_dev, first, width), preferred_element_type=F32)


def pick(heads_dev, first, width):
    row = lax.broadcasted_iota(jnp.int32, (LANES, width), 0)
    col = lax.broadcasted_iota(jnp.int32, (LANES, width), 1)
    head = first + col // HEADDIM
    hit = (row == head) | (row == head + heads_dev)
    return jnp.where(hit, 1.0, 0.0).astype(BF16)


def pack_bc(me, bc_in, dt_raw, n, heads_dev, per_group):
    tok = bc_in.shape[0]

    def body(me_ref, *refs):
        b_refs, c_refs, dt_ref = refs[:n], refs[n : 2 * n], refs[2 * n]
        outs, turned = refs[2 * n + 1 : 3 * n + 1], refs[3 * n + 1]
        turned[...] = dt_ref[...].astype(F32).T
        for s in range(n):
            outs[s][:tok, :STATE] = b_refs[s][...]
            outs[s][:tok, STATE:] = c_refs[s][...]
            first = pl.multiple_of(((me_ref[0] + s) % n) * heads_dev, heads_dev)
            dt_s = turned[pl.ds(first, heads_dev), :].astype(BF16)
            for seg in range(2):
                if seg * SEG < heads_dev:
                    part = dt_s[seg * SEG : (seg + 1) * SEG]
                else:
                    part = jnp.zeros((SEG, tok), BF16)
                outs[s][tok:, seg * tok : (seg + 1) * tok] = part

    def column(s, base):
        return lambda i, me: (0, base + ((me[0] + s) % n) * heads_dev // per_group)

    rows = tok + SEG
    return pl.pallas_call(
        body,
        grid_spec=pltpu.PrefetchScalarGridSpec(
            num_scalar_prefetch=1,
            grid=(1,),
            in_specs=[pl.BlockSpec((tok, STATE), column(s, 0)) for s in range(n)]
            + [pl.BlockSpec((tok, STATE), column(s, GROUPS)) for s in range(n)]
            + [whole(dt_raw.shape)],
            out_specs=[whole((rows, 2 * STATE))] * n,
            scratch_shapes=[pltpu.VMEM(dt_raw.shape[::-1], F32)],
        ),
        out_shape=[jax.ShapeDtypeStruct((rows, 2 * STATE), BF16)] * n,
        compiler_params=params(),
        cost_estimate=cost(0, 4 * bc_in.size),
        name="pack_bc",
    )(me, *([bc_in] * (2 * n)), dt_raw)


def pack_x(me, x_in, n, channels, width, first, after):
    tok = x_in.shape[0]
    step = min(64, tok)
    per = channels // width

    def body(me_ref, *refs):
        outs = refs[n - 1 + len(after) :]
        for s in range(n - 1):
            outs[s][...] = refs[s][...]

    def column(s):
        return lambda i, me: (i, ((me[0] + s) % n) * per + first // width)

    return pl.pallas_call(
        body,
        grid_spec=pltpu.PrefetchScalarGridSpec(
            num_scalar_prefetch=1,
            grid=(tok // step,),
            in_specs=[pl.BlockSpec((step, width), column(s)) for s in range(1, n)]
            + [ANY] * len(after),
            out_specs=[pl.BlockSpec((step, width), lambda i, me: (i, 0))] * (n - 1),
        ),
        out_shape=[jax.ShapeDtypeStruct((tok, width), BF16)] * (n - 1),
        compiler_params=params(),
        cost_estimate=cost(0, 4 * tok * width * (n - 1)),
        name="pack_x",
    )(me, *([x_in] * (n - 1)), *after)


def pack_edge(x_in, bc_in, n, channels, heads_dev, per_group):
    tok = x_in.shape[0]
    wide = channels + 2 * STATE

    def body(x_ref, bc_ref, *outs):
        x = x_ref[...].astype(F32)[2 * EDGE_ROWS - SENT_ROWS :].astype(BF16)
        bc = bc_ref[...].astype(F32)[2 * EDGE_ROWS - SENT_ROWS :].astype(BF16)
        for j in range(n):
            g = j * heads_dev // per_group
            outs[j][:, :channels] = x[:, j * channels : (j + 1) * channels]
            outs[j][:, channels : channels + STATE] = bc[:, g * STATE : (g + 1) * STATE]
            g += GROUPS
            outs[j][:, channels + STATE :] = bc[:, g * STATE : (g + 1) * STATE]

    last = tok // (2 * EDGE_ROWS) - 1
    return pl.pallas_call(
        body,
        grid=(1,),
        in_specs=[
            pl.BlockSpec((2 * EDGE_ROWS, x_in.shape[1]), lambda i: (last, 0)),
            pl.BlockSpec((2 * EDGE_ROWS, bc_in.shape[1]), lambda i: (last, 0)),
        ],
        out_specs=[whole((SENT_ROWS, wide))] * n,
        out_shape=[jax.ShapeDtypeStruct((SENT_ROWS, wide), BF16)] * n,
        compiler_params=params(),
        cost_estimate=cost(0, 4 * EDGE_ROWS * wide * n),
        name="pack_edge",
    )(x_in, bc_in)


def prepare(me, messages, edge, weight, bias, dt_bias, a_log, n, heads_dev, per_group):
    rows = messages[0].shape[0]
    tok = rows - SEG
    total = n * tok

    def body(me_ref, *refs):
        msgs, refs = refs[:n], refs[n:]
        edge_ref, wb_ref, wc_ref, bb_ref, bc_ref, dtb_ref, al_ref = refs[:7]
        bt_out, c_out, m_out, wu_out, wv_out, ec_out, dv_out = refs[7:14]
        buf, cum_s, dt_s, sems = refs[14:]
        copies = []
        for s in range(n):
            j = lax.rem(me_ref[0] - s + n, n)
            copies.append(pltpu.make_async_copy(msgs[s], buf.at[j], sems.at[s]))
            copies[-1].start()
        for copy in copies:
            copy.wait()

        def split(w):
            hi = w.astype(BF16).astype(F32)
            parts = [hi, w - hi]
            if 2 * heads_dev < LANES:
                parts.append(jnp.zeros((LANES - 2 * heads_dev, w.shape[1]), F32))
            return jnp.concatenate(parts, axis=0)

        at = lax.broadcasted_iota(jnp.int32, (tok, tok), 0)
        to = lax.broadcasted_iota(jnp.int32, (tok, tok), 1)
        upto = jnp.where(at <= to, 1.0, 0.0).astype(F32)
        rate = -jnp.exp(al_ref[...])
        ends = []
        for j in range(n):
            dt_raw = buf[j, tok:, :].astype(F32)
            segs = [dt_raw[:, i * tok : (i + 1) * tok] for i in range(heads_dev // SEG)]
            dt = jax.nn.softplus(jnp.concatenate(segs, axis=0) + dtb_ref[...])
            cum = jnp.dot(
                dt * rate,
                upto,
                precision=lax.Precision.HIGHEST,
                preferred_element_type=F32,
            )
            dt_s[j] = dt
            cum_s[j] = cum
            ends.append(cum[:, tok - 1 :])
        after = jnp.zeros_like(ends[0])
        for j in reversed(range(n)):
            dt, cum = dt_s[j], cum_s[j]
            here = pl.ds(j * tok, tok)
            wu_out[here, :] = split(dt * jnp.exp(-cum)).T.astype(BF16)
            wv_out[here, :] = split(dt * jnp.exp(after + ends[j] - cum)).T.astype(BF16)
            ec_out[here, :] = split(jnp.exp(cum)).T.astype(BF16)
            after = after + ends[j]
        decay = jnp.broadcast_to(jnp.exp(after), (heads_dev, LANES))
        dv_out[...] = split(decay).T.astype(BF16)[: dv_out.shape[0]]

        strip = 32
        lower = at >= to

        def block(j, carry):
            def step(i, carry):
                r = pl.multiple_of(i * strip, strip)
                x = buf[j, pl.ds(r, strip), :].astype(F32)
                new = []
                for half, w_ref, b_ref in ((0, wb_ref, bb_ref), (1, wc_ref, bc_ref)):
                    mine = x[:, half * STATE : (half + 1) * STATE]
                    done = conv_rows(carry[half], mine, w_ref[...], b_ref[...])
                    buf[j, pl.ds(r, strip), half * STATE : (half + 1) * STATE] = done
                    new.append(mine[strip - EDGE_ROWS :])
                return tuple(new)

            carry = lax.fori_loop(0, tok // strip, step, carry)
            b, c = buf[j, :tok, :STATE], buf[j, :tok, STATE:]
            t = pl.multiple_of(j * tok, tok)
            turned = b.astype(F32).T.astype(BF16)
            bt_out[:, pl.ds(t, tok)] = turned
            c_out[pl.ds(t, tok), :] = c
            scores = jnp.dot(c, turned, preferred_element_type=F32)
            m_out[pl.ds(t, tok), :] = jnp.where(lower, scores, 0.0).astype(BF16)
            return carry

        e = rows_ahead(edge_ref)
        lax.fori_loop(0, n, block, (e[:, :STATE], e[:, STATE:]))

    def group(base):
        return lambda i, me: (0, base + me[0] * heads_dev // per_group)

    vec = (heads_dev, 1)
    shapes = [
        (STATE, total),
        (total, STATE),
        (total, tok),
        (total, LANES),
        (total, LANES),
        (total, LANES),
        (2 * EDGE_ROWS, LANES),
    ]
    return pl.pallas_call(
        body,
        grid_spec=pltpu.PrefetchScalarGridSpec(
            num_scalar_prefetch=1,
            grid=(1,),
            in_specs=[ANY] * n
            + [
                whole(edge.shape),
                pl.BlockSpec((CONV, STATE), group(0)),
                pl.BlockSpec((CONV, STATE), group(GROUPS)),
                pl.BlockSpec((1, STATE), group(0)),
                pl.BlockSpec((1, STATE), group(GROUPS)),
                whole(vec),
                whole(vec),
            ],
            out_specs=[whole(s) for s in shapes],
            scratch_shapes=[
                pltpu.VMEM((n, rows, 2 * STATE), BF16),
                pltpu.VMEM((n, heads_dev, tok), F32),
                pltpu.VMEM((n, heads_dev, tok), F32),
                pltpu.SemaphoreType.DMA((n,)),
            ],
        ),
        out_shape=[jax.ShapeDtypeStruct(s, BF16) for s in shapes],
        compiler_params=params(),
        cost_estimate=cost(4 * total * STATE * tok, 20 * total * STATE),
        name="prepare",
    )(me, *messages, edge, weight, weight, bias, bias, dt_bias, a_log)


def convolve(me, x_in, received, edge, weight, bias, bt, wv, n, heads_dev, channels, width, first, after):
    tok = x_in.shape[0]
    total = n * tok
    per = channels // width
    group = min(width, 256)
    strip = min(tok, 64 * 256 // group)

    def body(me_ref, x_ref, *refs):
        got, refs = refs[: n - 1], refs[n - 1 :]
        edge_ref, w_ref, b_ref, bt_ref, wv_ref = refs[:5]
        xc_ref, end_out, buf, scale, end_ref, sems, out_sems = refs[5 + len(after) :]
        copies = []
        for s in range(n):
            j = lax.rem(me_ref[0] - s + n, n)
            if s:
                src = got[s - 1]
            else:
                col = pl.multiple_of(me_ref[0] * channels + first, LANES)
                src = x_ref.at[:, pl.ds(col, width)]
            copies.append(pltpu.make_async_copy(src, buf.at[j], sems.at[s]))
            copies[-1].start()
        for copy in copies:
            copy.wait()
        end_ref[...] = jnp.zeros_like(end_ref)

        def block(j, carry):
            t = pl.multiple_of(j * tok, tok)
            scale[...] = spread(wv_ref[pl.ds(t, tok), :], heads_dev, first // HEADDIM, width)

            def step(i, carry):
                r = pl.multiple_of(i * strip, strip)
                new = []
                for g in range(width // group):
                    cols = slice(g * group, (g + 1) * group)
                    x = buf[j, pl.ds(r, strip), cols].astype(F32)
                    xc = conv_rows(carry[g], x, w_ref[:, cols], b_ref[:, cols])
                    buf[j, pl.ds(r, strip), cols] = xc
                    v = xc.astype(F32) * scale[pl.ds(r, strip), cols]
                    scale[pl.ds(r, strip), cols] = v
                    new.append(x[strip - EDGE_ROWS :])
                return tuple(new)

            carry = lax.fori_loop(0, tok // strip, step, carry)
            pltpu.make_async_copy(buf.at[j], xc_ref.at[pl.ds(t, tok), :], out_sems.at[j]).start()
            lhs = bt_ref[:, pl.ds(t, tok)]
            for g in range(width // group):
                cols = slice(g * group, (g + 1) * group)
                v = scale[:, cols].astype(BF16)
                end_ref[:, cols] += jnp.dot(lhs, v, preferred_element_type=F32)
            return carry

        e = rows_ahead(edge_ref)
        lax.fori_loop(
            0, n, block, tuple(e[:, g * group : (g + 1) * group] for g in range(width // group))
        )
        end_out[...] = end_ref[...].astype(BF16)
        for j in range(n):
            pltpu.make_async_copy(
                buf.at[j], xc_ref.at[pl.ds(j * tok, tok), :], out_sems.at[j]
            ).wait()

    return pl.pallas_call(
        body,
        grid_spec=pltpu.PrefetchScalarGridSpec(
            num_scalar_prefetch=1,
            grid=(1,),
            in_specs=[ANY] * n
            + [
                pl.BlockSpec((SENT_ROWS, width), lambda i, me: (0, first // width)),
                pl.BlockSpec((CONV, width), lambda i, me: (0, me[0] * per + first // width)),
                pl.BlockSpec((1, width), lambda i, me: (0, me[0] * per + first // width)),
                whole(bt.shape),
                whole(wv.shape),
            ]
            + [ANY] * len(after),
            out_specs=[ANY, whole((STATE, width))],
            scratch_shapes=[
                pltpu.VMEM((n, tok, width), BF16),
                pltpu.VMEM((tok, width), F32),
                pltpu.VMEM((STATE, width), F32),
                pltpu.SemaphoreType.DMA((n,)),
                pltpu.SemaphoreType.DMA((n,)),
            ],
        ),
        out_shape=[
            jax.ShapeDtypeStruct((total, width), BF16),
            jax.ShapeDtypeStruct((STATE, width), BF16),
        ],
        compiler_params=params(),
        cost_estimate=cost(2 * total * STATE * width, 4 * total * width + 4 * total * STATE),
        name="convolve",
    )(me, x_in, *received, edge, weight, bias, bt, wv, *after)


def emit(y, xc, bt, c, m, wu, ec, ends, decays, skip, heads_dev, channels, width, first):
    total = xc.shape[0]
    tok = m.shape[1]
    group = min(width, 256)
    n_ends, n_decays = len(ends), len(decays)
    alias = [] if y is None else [y]

    def body(*refs):
        refs = refs[len(alias) :]
        xc_ref, bt_ref, c_ref, m_ref, wu_ref, ec_ref, skip_ref = refs[:7]
        end_refs, refs = refs[7 : 7 + n_ends], refs[7 + n_ends :]
        decay_refs, (out_ref, token_ref, state) = refs[:n_decays], refs[n_decays:]

        @pl.when(pl.program_id(0) == 0)
        def _():
            carried = end_refs[-1][...].astype(F32)
            for i in reversed(range(n_ends - 1)):
                d = spread(decay_refs[i][...], heads_dev, first // HEADDIM, width)[:1]
                carried = end_refs[i][...].astype(F32) + d * carried
            state[...] = carried
            token_ref[...] = jnp.zeros_like(token_ref)

        for g in range(width // group):
            cols = slice(g * group, (g + 1) * group)
            head = first // HEADDIM + g * (group // HEADDIM)
            x = xc_ref[:, cols].astype(F32)
            u = (x * spread(wu_ref[...], heads_dev, head, group)).astype(BF16)
            e = spread(ec_ref[...], heads_dev, head, group)
            s = state[:, cols]
            y_g = jnp.dot(m_ref[...], u, preferred_element_type=F32)
            y_g += jnp.dot(c_ref[...], s.astype(BF16), preferred_element_type=F32)
            out_ref[:, cols] = (e * y_g + skip_ref[:, cols] * x).astype(BF16)
            s = s + jnp.dot(bt_ref[...], u, preferred_element_type=F32)
            state[:, cols] = e[tok - 1 :] * s

    row = lambda j: (j, 0)
    return pl.pallas_call(
        body,
        grid=(total // tok,),
        in_specs=[ANY] * len(alias)
        + [
            pl.BlockSpec((tok, width), row),
            pl.BlockSpec((STATE, tok), lambda j: (0, j)),
            pl.BlockSpec((tok, STATE), row),
            pl.BlockSpec((tok, tok), row),
            pl.BlockSpec((tok, LANES), row),
            pl.BlockSpec((tok, LANES), row),
            pl.BlockSpec((1, width), lambda j: (0, first // width)),
        ]
        + [whole((STATE, width))] * n_ends
        + [whole((2 * EDGE_ROWS, LANES))] * n_decays,
        out_specs=[
            pl.BlockSpec((tok, width), lambda j: (j, first // width)),
            whole((EDGE_ROWS, LANES)),
        ],
        out_shape=[
            jax.ShapeDtypeStruct((total, channels), BF16),
            jax.ShapeDtypeStruct((EDGE_ROWS, LANES), F32),
        ],
        scratch_shapes=[pltpu.VMEM((STATE, width), F32)],
        input_output_aliases={0: 0} if alias else {},
        compiler_params=params(),
        cost_estimate=cost(6 * total * STATE * width, 4 * total * width + 6 * total * STATE),
        name="emit",
    )(*alias, xc, bt, c, m, wu, ec, skip, *ends, *decays)


def shards(
    x_in,
    bc_in,
    dt_raw,
    dt_bias,
    a_log,
    d_skip,
    conv_x_weight,
    conv_x_bias,
    conv_bc_weight,
    conv_bc_bias,
):
    n = lax.axis_size("inner")
    n_slab = lax.axis_size("slab")
    heads_dev = HEADS // n
    channels = heads_dev * HEADDIM
    per_group = HEADS // GROUPS
    index = lax.axis_index("inner")
    me = index.astype(jnp.int32).reshape(1)

    middle = n // 2
    shifts = sorted(range(1, n), key=lambda s: abs(s - middle))

    def rotate(arrays, chosen):
        for s in chosen:
            arrays[s - 1] = lax.ppermute(
                arrays[s - 1], "inner", [(i, (i + s) % n) for i in range(n)]
            )

    def forward(a, by):
        return lax.ppermute(a, "slab", [(i, i + by) for i in range(n_slab - by)])

    def mine(v):
        return lax.dynamic_slice_in_dim(v, index * heads_dev, heads_dev, 0)

    def send(k, after):
        width, first = widths[k], sum(widths[:k])
        parts = list(pack_x(me, x_in, n, channels, width, first, after))
        rotate(parts, shifts[1:2])
        rotate(parts, shifts[:1] + shifts[2:])
        return parts

    widths = chunk_widths(channels)
    packed = list(pack_bc(me, bc_in, dt_raw, n, heads_dev, per_group))
    messages = packed[1:]
    rotate(messages, shifts)
    messages = packed[:1] + messages
    received = [send(k, []) for k in range(len(widths))]
    edges = pack_edge(x_in, bc_in, n, channels, heads_dev, per_group)
    edges = [
        lax.ppermute(
            e, ("slab", "inner"), [(s * n + n - 1, (s + 1) * n + j) for s in range(n_slab - 1)]
        )
        for j, e in enumerate(edges)
    ]
    edge = sum(edges)
    skip = jnp.repeat(mine(d_skip), HEADDIM)[None, :]
    bt, c, m, wu, wv, ec, dv = prepare(
        me,
        messages,
        edge[:, channels:],
        conv_bc_weight,
        conv_bc_bias[None, :],
        mine(dt_bias)[:, None],
        mine(a_log)[:, None],
        n,
        heads_dev,
        per_group,
    )
    decays = [forward(dv, by) for by in range(1, n_slab - 1)]
    y = None
    tokens, pending = [], []

    def finish():
        k, xc, ends = pending.pop(0)
        return emit(
            y,
            xc,
            bt,
            c,
            m,
            wu,
            ec,
            ends,
            decays,
            skip,
            heads_dev,
            channels,
            widths[k],
            sum(widths[:k]),
        )

    last = len(widths) - 1
    for k, width in enumerate(widths):
        xc, end = convolve(
            me,
            x_in,
            received[k],
            edge,
            conv_x_weight,
            conv_x_bias[None, :],
            bt,
            wv,
            n,
            heads_dev,
            channels,
            width,
            sum(widths[:k]),
            decays if k == 0 else tokens[-1:],
        )
        ends = [forward(end, by) for by in range(1, n_slab)]
        pending.append((k, xc, ends))
        while pending and (len(pending) > 1 or k >= last - 1):
            y, token = finish()
            tokens.append(token)
    return y


def solution(mesh):
    tokens = P(("slab", "inner"), None)
    placed = (tokens, tokens, tokens) + (P(),) * 7

    return jax.shard_map(
        shards, mesh=mesh, in_specs=placed, out_specs=P("slab", "inner"), check_vma=False
    )
```

profile of v0, /device:TPU:15, one launch (start us, length us, event | category | flops | bytes accessed | tf_op | source)
XLA Modules:
  0.0 333.7 jit_solution(10836381867070413243)
XLA Ops:
  0.0 3.8 %pack_x.4 = (bf16[256,512]{1,0:T(8,128)(2,1)}, bf16[256,512]{1,0:T(8,128)(2,1)}, bf16[256,512]{1,0:T(8,128)(2,1)}, bf16[256,512]{1,0:T(8,128)(2,1)}, bf16[256,51...) custom-call(s32[1]{0:T(128)} %bitcast.me_ref, bf16[256,16384]{1,0:T(8,128)(2,1)} %x_ref.9, ...), custom_call_target="tpu_custom_call" | custom-call | bytes 3670016 | tf_op jit(solution)/shard_map/pack_x/pallas_call | solution.py:126
  3.8 1.3 collective-permute-start
  5.1 1.3 collective-permute-start.1
  6.4 0.9 collective-permute-start.2
  7.3 1.3 collective-permute-start.3
  8.7 1.8 pack_edge.1
  13.1 1.3 collective-permute-start.10
  14.4 21.4 %collective-permute-done.10 = bf16[4,2560]{1,0:T(4,128)(2,1)S(1)} collective-permute-done((bf16[4,2560]{1,0:T(4,128)(2,1)}, bf16[4,2560]{1,0:T(4,128)(2,1)S(1)}, u32[]{:S(2)}, u32[]{:S(2)}) %collective-permute-start.10) | collective-permute-done | bytes 20512 | tf_op jit(solution)/shard_map/ppermute | solution.py:508
  37.9 6.8 %collective-permute-start.4 = (bf16[256,512]{1,0:T(8,128)(2,1)}, bf16[256,512]{1,0:T(8,128)(2,1)}, u32[]{:S(2)}, u32[]{:S(2)}) collective-permute-start(bf16[256,512]{1,0:T(8,128)(2,1)} %get-tuple-element.74), channel_id=1, source_target_pairs={{0,5},{1,6},{2,7},{3,0},{4,1},{5,2},{6,3},{7,4},{8,13},{9,14},{10,... | collective-permute-start | bytes 786440 | tf_op jit(solution)/shard_map/ppermute | solution.py:483
  44.7 1.8 collective-permute-start.5
  46.6 3.7 %pack_x.5 = (bf16[256,512]{1,0:T(8,128)(2,1)}, bf16[256,512]{1,0:T(8,128)(2,1)}, bf16[256,512]{1,0:T(8,128)(2,1)}, bf16[256,512]{1,0:T(8,128)(2,1)}, bf16[256,51...) custom-call(s32[1]{0:T(128)} %bitcast.me_ref, bf16[256,16384]{1,0:T(8,128)(2,1)} %x_ref.9, ...), custom_call_target="tpu_custom_call" | custom-call | bytes 3670016 | tf_op jit(solution)/shard_map/pack_x/pallas_call | solution.py:126
  50.4 2.3 collective-permute-start.27
  53.5 3.2 pack_bc.1
  56.7 1.4 collective-permute-start.15
  58.1 8.2 %collective-permute-done.5.refs_5_ = bf16[256,512]{1,0:T(8,128)(2,1)} collective-permute-done((bf16[256,512]{1,0:T(8,128)(2,1)}, bf16[256,512]{1,0:T(8,128)(2,1)}, u32[]{:S(2)}, u32[]{:S(2)}) %collective-permute-start.5) | collective-permute-done | bytes 262176 | tf_op jit(solution)/shard_map/ppermute | solution.py:483
  66.3 16.1 %collective-permute-done.6.refs_6_ = bf16[256,512]{1,0:T(8,128)(2,1)} collective-permute-done((bf16[256,512]{1,0:T(8,128)(2,1)}, bf16[256,512]{1,0:T(8,128)(2,1)}, u32[]{:S(2)}, u32[]{:S(2)}) %collective-permute-start.6) | collective-permute-done | bytes 262176 | tf_op jit(solution)/shard_map/ppermute | solution.py:483
  82.4 2.4 collective-permute-start.31
  84.8 24.4 %collective-permute-done.29.refs_2_ = bf16[256,512]{1,0:T(8,128)(2,1)S(1)} collective-permute-done((bf16[256,512]{1,0:T(8,128)(2,1)}, bf16[256,512]{1,0:T(8,128)(2,1)S(1)}, u32[]{:S(2)}, u32[]{:S(2)}) %collective-permute-start.29) | collective-permute-done | bytes 262176 | tf_op jit(solution)/shard_map/ppermute | solution.py:483
  109.2 3.6 %collective-permute-start.17 = (bf16[272,512]{1,0:T(8,128)(2,1)}, bf16[272,512]{1,0:T(8,128)(2,1)S(1)}, u32[]{:S(2)}, u32[]{:S(2)}) collective-permute-start(bf16[272,512]{1,0:T(8,128)(2,1)} %get-tuple-element.88), channel_id=1, source_target_pairs={{0,3},{1,4},{2,5},{3,6},{4,7},{5,0},{6,1},{7,2},{8,11},{9,12},{10,... | collective-permute-start | bytes 835592 | tf_op jit(solution)/shard_map/ppermute | solution.py:483
  112.8 19.7 %collective-permute-done.30.refs_3_ = bf16[256,512]{1,0:T(8,128)(2,1)S(1)} collective-permute-done((bf16[256,512]{1,0:T(8,128)(2,1)}, bf16[256,512]{1,0:T(8,128)(2,1)S(1)}, u32[]{:S(2)}, u32[]{:S(2)}) %collective-permute-start.30) | collective-permute-done | bytes 262176 | tf_op jit(solution)/shard_map/ppermute | solution.py:483
  132.6 2.7 collective-permute-start.18
  136.7 3.8 %pack_x.6 = (bf16[256,512]{1,0:T(8,128)(2,1)}, bf16[256,512]{1,0:T(8,128)(2,1)}, bf16[256,512]{1,0:T(8,128)(2,1)}, bf16[256,512]{1,0:T(8,128)(2,1)}, bf16[256,51...) custom-call(s32[1]{0:T(128)} %bitcast.me_ref, bf16[256,16384]{1,0:T(8,128)(2,1)} %x_ref.9, ...), custom_call_target="tpu_custom_call" | custom-call | bytes 3670016 | tf_op jit(solution)/shard_map/pack_x/pallas_call | solution.py:126
  142.7 3.5 %collective-permute-start.32 = (bf16[256,512]{1,0:T(8,128)(2,1)}, bf16[256,512]{1,0:T(8,128)(2,1)S(1)}, u32[]{:S(2)}, u32[]{:S(2)}) collective-permute-start(bf16[256,512]{1,0:T(8,128)(2,1)} %get-tuple-element.108), channel_id=1, source_target_pairs={{0,6},{1,7},{2,0},{3,1},{4,2},{5,3},{6,4},{7,5},{8,14},{9,15},{10,... | collective-permute-start | bytes 786440 | tf_op jit(solution)/shard_map/ppermute | solution.py:483
  146.2 2.3 collective-permute-start.37
  148.5 7.2 %collective-permute-done.21.refs_7_ = bf16[272,512]{1,0:T(8,128)(2,1)} collective-permute-done((bf16[272,512]{1,0:T(8,128)(2,1)}, bf16[272,512]{1,0:T(8,128)(2,1)}, u32[]{:S(2)}, u32[]{:S(2)}) %collective-permute-start.21) | collective-permute-done | bytes 278560 | tf_op jit(solution)/shard_map/ppermute | solution.py:483
  155.7 3.4 %collective-permute-start.39 = (bf16[256,512]{1,0:T(8,128)(2,1)}, bf16[256,512]{1,0:T(8,128)(2,1)}, u32[]{:S(2)}, u32[]{:S(2)}) collective-permute-start(bf16[256,512]{1,0:T(8,128)(2,1)} %get-tuple-element.115), channel_id=1, source_target_pairs={{0,3},{1,4},{2,5},{3,6},{4,7},{5,0},{6,1},{7,2},{8,11},{9,12},{10,... | collective-permute-start | bytes 786440 | tf_op jit(solution)/shard_map/ppermute | solution.py:483
  159.1 0.8 add_add_fusion.refs_7_
  160.5 11.9 %prepare.1 = (bf16[256,2048]{1,0:T(8,128)(2,1)}, bf16[2048,256]{1,0:T(8,128)(2,1)}, bf16[2048,256]{1,0:T(8,128)(2,1)}, bf16[2048,128]{1,0:T(8,128)(2,1)}, bf16[2...) custom-call(s32[1]{0:T(128)} %bitcast.me_ref, ...), custom_call_target="tpu_custom_call" | custom-call | flops 536870912 | bytes 10485760 | tf_op jit(solution)/shard_map/prepare/pallas_call | solution.py:267
  172.4 1.3 collective-permute-start.22
  174.2 1.3 collective-permute-start.23
  175.7 3.3 collective-permute-done.23.refs_13_.refs_11_.refs_12_
  179.6 11.3 %convolve.4 = (bf16[2048,512]{1,0:T(8,128)(2,1)}, bf16[256,512]{1,0:T(8,128)(2,1)}) custom-call(s32[1]{0:T(128)} %bitcast.me_ref, bf16[256,16384]{1,0:T(8,128)(2,1)} %x_ref.9, bf16[256,512]{1,0:T(8,128)(2,1)} %copy-done.13, bf16[256,512]{1,0:T(8,128)(2,1)} %copy-done.14, bf16[256,512]{1,0:T(8,128)(2,1)} %copy-done.15, ...), custom_call_target="tpu_custom_call" | custom-call | flops 536870912 | bytes 6291456 | tf_op jit(solution)/shard_map/convolve/pallas_call | solution.py:358
  191.7 1.3 collective-permute-start.24
  193.0 1.3 collective-permute-start.25
  194.3 1.3 collective-permute-start.26
  196.3 2.0 collective-permute-start.43
  198.3 3.8 %pack_x.7 = (bf16[256,512]{1,0:T(8,128)(2,1)}, bf16[256,512]{1,0:T(8,128)(2,1)}, bf16[256,512]{1,0:T(8,128)(2,1)}, bf16[256,512]{1,0:T(8,128)(2,1)}, bf16[256,51...) custom-call(s32[1]{0:T(128)} %bitcast.me_ref, bf16[256,16384]{1,0:T(8,128)(2,1)} %x_ref.9, ...), custom_call_target="tpu_custom_call" | custom-call | bytes 3670016 | tf_op jit(solution)/shard_map/pack_x/pallas_call | solution.py:126
  202.6 11.3 %convolve.5 = (bf16[2048,512]{1,0:T(8,128)(2,1)}, bf16[256,512]{1,0:T(8,128)(2,1)}) custom-call(s32[1]{0:T(128)} %bitcast.me_ref, bf16[256,16384]{1,0:T(8,128)(2,1)} %x_ref.9, bf16[256,512]{1,0:T(8,128)(2,1)} %collective-permute-done.27.refs_0_, bf16[256,512]{1,0:T(8,128)(2,1)} %collective-permute-done.28.refs_1_, bf16[256,512]{1,0:T(8,128)(2,1)} %copy-done.16, ...), custom_call_target="tpu_custom_call" | custom-call | flops 536870912 | bytes 6291456 | tf_op jit(solution)/shard_map/convolve/pallas_call | solution.py:358
  213.9 0.8 collective-permute-start.48
  215.5 1.3 collective-permute-start.34
  217.6 9.8 %emit.4 = (bf16[2048,2048]{1,0:T(8,128)(2,1)}, f32[8,128]{1,0:T(8,128)}) custom-call(bf16[2048,512]{1,0:T(8,128)(2,1)} %get-tuple-element.96.refs_0_, bf16[256,2048]{1,0:T(8,128)(2,1)} %get-tuple-element.93.refs_10_.refs_1_.refs_2_, bf16[2048,256]{1,0:T(8,128)(2,1)} %get-tuple-element.97.refs_2_.refs_3_, ...), custom_call_target="tpu_custom_call" | custom-call | flops 1610612736 | bytes 7340032 | tf_op jit(solution)/shard_map/emit/pallas_call | solution.py:427
  227.4 1.3 collective-permute-start.35
  228.7 1.3 collective-permute-start.36
  230.0 11.4 %convolve.6 = (bf16[2048,512]{1,0:T(8,128)(2,1)}, bf16[256,512]{1,0:T(8,128)(2,1)}) custom-call(s32[1]{0:T(128)} %bitcast.me_ref, bf16[256,16384]{1,0:T(8,128)(2,1)} %x_ref.9, bf16[256,512]{1,0:T(8,128)(2,1)} %copy-done.19, bf16[256,512]{1,0:T(8,128)(2,1)} %collective-permute-done.38.refs_1_, bf16[256,512]{1,0:T(8,128)(2,1)} %collective-permute-done.39.refs_2_, ...), custom_call_target="tpu_custom_call" | custom-call | flops 536870912 | bytes 6291456 | tf_op jit(solution)/shard_map/convolve/pallas_call | solution.py:358
  241.4 1.3 collective-permute-start.44
  242.7 1.3 collective-permute-start.45
  244.0 1.3 collective-permute-start.46
  245.4 5.9 %collective-permute-start.49 = (bf16[256,512]{1,0:T(8,128)(2,1)}, bf16[256,512]{1,0:T(8,128)(2,1)}, u32[]{:S(2)}, u32[]{:S(2)}) collective-permute-start(bf16[256,512]{1,0:T(8,128)(2,1)} %get-tuple-element.126), channel_id=1, source_target_pairs={{0,3},{1,4},{2,5},{3,6},{4,7},{5,0},{6,1},{7,2},{8,11},{9,12},{10,... | collective-permute-start | bytes 786440 | tf_op jit(solution)/shard_map/ppermute | solution.py:483
  251.4 2.3 collective-permute-start.51
  253.7 3.8 %collective-permute-done.45.refs_9_ = bf16[256,512]{1,0:T(8,128)(2,1)} collective-permute-done((bf16[256,512]{1,0:T(8,128)(2,1)}, bf16[256,512]{1,0:T(8,128)(2,1)}, u32[]{:S(2)}, u32[]{:S(2)}) %collective-permute-start.45) | collective-permute-done | bytes 262176 | tf_op jit(solution)/shard_map/ppermute | solution.py:488
  257.5 2.4 collective-permute-start.52
  260.4 1.3 collective-permute-start.53
  261.7 9.9 %emit.5 = (bf16[2048,2048]{1,0:T(8,128)(2,1)}, f32[8,128]{1,0:T(8,128)}) custom-call(bf16[2048,2048]{1,0:T(8,128)(2,1)} %get-tuple-element.102.refs_0_, bf16[2048,512]{1,0:T(8,128)(2,1)} %get-tuple-element.110.refs_1_, bf16[256,2048]{1,0:T(8,128)(2,1)} %get-tuple-element.93.refs_10_.refs_1_.refs_2_, ...), custom_call_target="tpu_custom_call", output_to_operand_aliasing={{0}: (0, {})} | custom-call | flops 1610612736 | bytes 7340032 | tf_op jit(solution)/shard_map/emit/pallas_call | solution.py:427
  271.6 9.9 %emit.6 = (bf16[2048,2048]{1,0:T(8,128)(2,1)}, f32[8,128]{1,0:T(8,128)}) custom-call(bf16[2048,2048]{1,0:T(8,128)(2,1)} %get-tuple-element.112.refs_0_, bf16[2048,512]{1,0:T(8,128)(2,1)} %get-tuple-element.121.refs_1_, bf16[256,2048]{1,0:T(8,128)(2,1)} %get-tuple-element.93.refs_10_.refs_1_.refs_2_, ...), custom_call_target="tpu_custom_call", output_to_operand_aliasing={{0}: (0, {})} | custom-call | flops 1610612736 | bytes 7340032 | tf_op jit(solution)/shard_map/emit/pallas_call | solution.py:427
  281.5 2.2 collective-permute-done.50.refs_3_
  283.7 2.8 collective-permute-done.52.refs_5_
  286.5 5.6 %collective-permute-done.53.refs_6_ = bf16[256,512]{1,0:T(8,128)(2,1)} collective-permute-done((bf16[256,512]{1,0:T(8,128)(2,1)}, bf16[256,512]{1,0:T(8,128)(2,1)}, u32[]{:S(2)}, u32[]{:S(2)}) %collective-permute-start.53) | collective-permute-done | bytes 262176 | tf_op jit(solution)/shard_map/ppermute | solution.py:483
  292.1 11.3 %convolve.7 = (bf16[2048,512]{1,0:T(8,128)(2,1)}, bf16[256,512]{1,0:T(8,128)(2,1)}) custom-call(s32[1]{0:T(128)} %bitcast.me_ref, bf16[256,16384]{1,0:T(8,128)(2,1)} %x_ref.9, bf16[256,512]{1,0:T(8,128)(2,1)} %collective-permute-done.47.refs_0_, bf16[256,512]{1,0:T(8,128)(2,1)} %collective-permute-done.48.refs_1_, ...), custom_call_target="tpu_custom_call" | custom-call | flops 536870912 | bytes 6291456 | tf_op jit(solution)/shard_map/convolve/pallas_call | solution.py:358
  303.4 1.3 collective-permute-start.54
  304.7 1.3 collective-permute-start.55
  306.0 1.3 collective-permute-start.56
  307.4 13.8 %collective-permute-done.55.refs_9_ = bf16[256,512]{1,0:T(8,128)(2,1)S(1)} collective-permute-done((bf16[256,512]{1,0:T(8,128)(2,1)}, bf16[256,512]{1,0:T(8,128)(2,1)S(1)}, u32[]{:S(2)}, u32[]{:S(2)}) %collective-permute-start.55) | collective-permute-done | bytes 262176 | tf_op jit(solution)/shard_map/ppermute | solution.py:488
  321.2 2.0 collective-permute-done.56.refs_10_
  323.8 9.9 %emit.7 = (bf16[2048,2048]{1,0:T(8,128)(2,1)}, f32[8,128]{1,0:T(8,128)}) custom-call(bf16[2048,2048]{1,0:T(8,128)(2,1)} %get-tuple-element.123.refs_0_, bf16[2048,512]{1,0:T(8,128)(2,1)} %get-tuple-element.132.refs_1_, bf16[256,2048]{1,0:T(8,128)(2,1)} %get-tuple-element.93.refs_10_.refs_1_.refs_2_, ...), custom_call_target="tpu_custom_call", output_to_operand_aliasing={{0}: (0, {})} | custom-call | flops 1610612736 | bytes 7340032 | tf_op jit(solution)/shard_map/emit/pallas_call | solution.py:427
  (125 shorter events, 15.7 us)
Async XLA Ops:
  3.8 41.0 %collective-permute-start = (bf16[256,512]{1,0:T(8,128)(2,1)}, bf16[256,512]{1,0:T(8,128)(2,1)S(1)}, u32[]{:S(2)}, u32[]{:S(2)}) collective-permute-start(bf16[256,512]{1,0:T(8,128)(2,1)} %get-tuple-element.70), channel_id=1, source_target_pairs={{0,1},{1,2},{2,3},{3,4},{4,5},{5,6},{6,7},{7,0},{8,9},{9,10},{10,1... | collective-permute-start | bytes 786440 | tf_op jit(solution)/shard_map/ppermute | solution.py:483
  5.1 45.2 %collective-permute-start.1 = (bf16[256,512]{1,0:T(8,128)(2,1)}, bf16[256,512]{1,0:T(8,128)(2,1)S(1)}, u32[]{:S(2)}, u32[]{:S(2)}) collective-permute-start(bf16[256,512]{1,0:T(8,128)(2,1)} %get-tuple-element.71), channel_id=1, source_target_pairs={{0,2},{1,3},{2,4},{3,5},{4,6},{5,7},{6,0},{7,1},{8,10},{9,11},{10,... | collective-permute-start | bytes 786440 | tf_op jit(solution)/shard_map/ppermute | solution.py:483
  6.4 44.0 %collective-permute-start.2 = (bf16[256,512]{1,0:T(8,128)(2,1)}, bf16[256,512]{1,0:T(8,128)(2,1)S(1)}, u32[]{:S(2)}, u32[]{:S(2)}) collective-permute-start(bf16[256,512]{1,0:T(8,128)(2,1)} %get-tuple-element.72), channel_id=1, source_target_pairs={{0,3},{1,4},{2,5},{3,6},{4,7},{5,0},{6,1},{7,2},{8,11},{9,12},{10,... | collective-permute-start | bytes 786440 | tf_op jit(solution)/shard_map/ppermute | solution.py:483
  7.3 45.5 %collective-permute-start.3 = (bf16[256,512]{1,0:T(8,128)(2,1)}, bf16[256,512]{1,0:T(8,128)(2,1)}, u32[]{:S(2)}, u32[]{:S(2)}) collective-permute-start(bf16[256,512]{1,0:T(8,128)(2,1)} %get-tuple-element.73), channel_id=1, source_target_pairs={{0,4},{1,5},{2,6},{3,7},{4,0},{5,1},{6,2},{7,3},{8,12},{9,13},{10,... | collective-permute-start | bytes 786440 | tf_op jit(solution)/shard_map/ppermute | solution.py:483
  10.4 0.7 collective-permute-start.14
  11.1 0.7 collective-permute-start.13
  11.8 0.7 collective-permute-start.12
  12.5 0.7 collective-permute-start.11
  13.1 22.7 %collective-permute-start.10 = (bf16[4,2560]{1,0:T(4,128)(2,1)}, bf16[4,2560]{1,0:T(4,128)(2,1)S(1)}, u32[]{:S(2)}, u32[]{:S(2)}) collective-permute-start(bf16[4,2560]{1,0:T(4,128)(2,1)} %get-tuple-element.80), channel_id=1, source_target_pairs={{7,11},{15,19},{23,27}} | collective-permute-start | bytes 61448 | tf_op jit(solution)/shard_map/ppermute | solution.py:508
  35.9 0.7 collective-permute-start.9
  36.5 0.7 collective-permute-start.7
  37.2 0.7 collective-permute-start.8
  37.9 18.8 %collective-permute-start.4 = (bf16[256,512]{1,0:T(8,128)(2,1)}, bf16[256,512]{1,0:T(8,128)(2,1)}, u32[]{:S(2)}, u32[]{:S(2)}) collective-permute-start(bf16[256,512]{1,0:T(8,128)(2,1)} %get-tuple-element.74), channel_id=1, source_target_pairs={{0,5},{1,6},{2,7},{3,0},{4,1},{5,2},{6,3},{7,4},{8,13},{9,14},{10,... | collective-permute-start | bytes 786440 | tf_op jit(solution)/shard_map/ppermute | solution.py:483
  44.7 21.6 %collective-permute-start.5 = (bf16[256,512]{1,0:T(8,128)(2,1)}, bf16[256,512]{1,0:T(8,128)(2,1)}, u32[]{:S(2)}, u32[]{:S(2)}) collective-permute-start(bf16[256,512]{1,0:T(8,128)(2,1)} %get-tuple-element.75), channel_id=1, source_target_pairs={{0,6},{1,7},{2,0},{3,1},{4,2},{5,3},{6,4},{7,5},{8,14},{9,15},{10,... | collective-permute-start | bytes 786440 | tf_op jit(solution)/shard_map/ppermute | solution.py:483
  50.3 32.1 %collective-permute-start.6 = (bf16[256,512]{1,0:T(8,128)(2,1)}, bf16[256,512]{1,0:T(8,128)(2,1)}, u32[]{:S(2)}, u32[]{:S(2)}) collective-permute-start(bf16[256,512]{1,0:T(8,128)(2,1)} %get-tuple-element.76), channel_id=1, source_target_pairs={{0,7},{1,0},{2,1},{3,2},{4,3},{5,4},{6,5},{7,6},{8,15},{9,8},{10,9... | collective-permute-start | bytes 786440 | tf_op jit(solution)/shard_map/ppermute | solution.py:483
  50.4 32.0 %collective-permute-start.27 = (bf16[256,512]{1,0:T(8,128)(2,1)}, bf16[256,512]{1,0:T(8,128)(2,1)}, u32[]{:S(2)}, u32[]{:S(2)}) collective-permute-start(bf16[256,512]{1,0:T(8,128)(2,1)} %get-tuple-element.103), channel_id=1, source_target_pairs={{0,1},{1,2},{2,3},{3,4},{4,5},{5,6},{6,7},{7,0},{8,9},{9,10},{10,1... | collective-permute-start | bytes 786440 | tf_op jit(solution)/shard_map/ppermute | solution.py:483
  52.8 29.7 %collective-permute-start.28 = (bf16[256,512]{1,0:T(8,128)(2,1)}, bf16[256,512]{1,0:T(8,128)(2,1)}, u32[]{:S(2)}, u32[]{:S(2)}) collective-permute-start(bf16[256,512]{1,0:T(8,128)(2,1)} %get-tuple-element.104), channel_id=1, source_target_pairs={{0,2},{1,3},{2,4},{3,5},{4,6},{5,7},{6,0},{7,1},{8,10},{9,11},{10,... | collective-permute-start | bytes 786440 | tf_op jit(solution)/shard_map/ppermute | solution.py:483
  56.7 78.6 %collective-permute-start.15 = (bf16[272,512]{1,0:T(8,128)(2,1)}, bf16[272,512]{1,0:T(8,128)(2,1)S(1)}, u32[]{:S(2)}, u32[]{:S(2)}) collective-permute-start(bf16[272,512]{1,0:T(8,128)(2,1)} %get-tuple-element.86), channel_id=1, source_target_pairs={{0,1},{1,2},{2,3},{3,4},{4,5},{5,6},{6,7},{7,0},{8,9},{9,10},{10,1... | collective-permute-start | bytes 835592 | tf_op jit(solution)/shard_map/ppermute | solution.py:483
  66.3 69.1 %collective-permute-start.16 = (bf16[272,512]{1,0:T(8,128)(2,1)}, bf16[272,512]{1,0:T(8,128)(2,1)S(1)}, u32[]{:S(2)}, u32[]{:S(2)}) collective-permute-start(bf16[272,512]{1,0:T(8,128)(2,1)} %get-tuple-element.87), channel_id=1, source_target_pairs={{0,2},{1,3},{2,4},{3,5},{4,6},{5,7},{6,0},{7,1},{8,10},{9,11},{10,... | collective-permute-start | bytes 835592 | tf_op jit(solution)/shard_map/ppermute | solution.py:483
  82.4 26.8 %collective-permute-start.29 = (bf16[256,512]{1,0:T(8,128)(2,1)}, bf16[256,512]{1,0:T(8,128)(2,1)S(1)}, u32[]{:S(2)}, u32[]{:S(2)}) collective-permute-start(bf16[256,512]{1,0:T(8,128)(2,1)} %get-tuple-element.105), channel_id=1, source_target_pairs={{0,3},{1,4},{2,5},{3,6},{4,7},{5,0},{6,1},{7,2},{8,11},{9,12},{10,... | collective-permute-start | bytes 786440 | tf_op jit(solution)/shard_map/ppermute | solution.py:483
  82.4 50.2 %collective-permute-start.30 = (bf16[256,512]{1,0:T(8,128)(2,1)}, bf16[256,512]{1,0:T(8,128)(2,1)S(1)}, u32[]{:S(2)}, u32[]{:S(2)}) collective-permute-start(bf16[256,512]{1,0:T(8,128)(2,1)} %get-tuple-element.106), channel_id=1, source_target_pairs={{0,4},{1,5},{2,6},{3,7},{4,0},{5,1},{6,2},{7,3},{8,12},{9,13},{10,... | collective-permute-start | bytes 786440 | tf_op jit(solution)/shard_map/ppermute | solution.py:483
  82.4 52.9 %collective-permute-start.31 = (bf16[256,512]{1,0:T(8,128)(2,1)}, bf16[256,512]{1,0:T(8,128)(2,1)S(1)}, u32[]{:S(2)}, u32[]{:S(2)}) collective-permute-start(bf16[256,512]{1,0:T(8,128)(2,1)} %get-tuple-element.107), channel_id=1, source_target_pairs={{0,5},{1,6},{2,7},{3,0},{4,1},{5,2},{6,3},{7,4},{8,13},{9,14},{10,... | collective-permute-start | bytes 786440 | tf_op jit(solution)/shard_map/ppermute | solution.py:483
  109.2 26.2 %copy-start.16 = (bf16[256,512]{1,0:T(8,128)(2,1)}, bf16[256,512]{1,0:T(8,128)(2,1)S(1)}, u32[]{:S(2)}) copy-start(bf16[256,512]{1,0:T(8,128)(2,1)S(1)} %collective-permute-done.29.refs_2_) | copy-start | bytes 786436
  109.2 33.4 %collective-permute-start.17 = (bf16[272,512]{1,0:T(8,128)(2,1)}, bf16[272,512]{1,0:T(8,128)(2,1)S(1)}, u32[]{:S(2)}, u32[]{:S(2)}) collective-permute-start(bf16[272,512]{1,0:T(8,128)(2,1)} %get-tuple-element.88), channel_id=1, source_target_pairs={{0,3},{1,4},{2,5},{3,6},{4,7},{5,0},{6,1},{7,2},{8,11},{9,12},{10,... | collective-permute-start | bytes 835592 | tf_op jit(solution)/shard_map/ppermute | solution.py:483
  132.6 13.5 %collective-permute-start.18 = (bf16[272,512]{1,0:T(8,128)(2,1)}, bf16[272,512]{1,0:T(8,128)(2,1)}, u32[]{:S(2)}, u32[]{:S(2)}) collective-permute-start(bf16[272,512]{1,0:T(8,128)(2,1)} %get-tuple-element.89), channel_id=1, source_target_pairs={{0,4},{1,5},{2,6},{3,7},{4,0},{5,1},{6,2},{7,3},{8,12},{9,13},{10,... | collective-permute-start | bytes 835592 | tf_op jit(solution)/shard_map/ppermute | solution.py:483
  135.3 10.8 %collective-permute-start.19 = (bf16[272,512]{1,0:T(8,128)(2,1)}, bf16[272,512]{1,0:T(8,128)(2,1)}, u32[]{:S(2)}, u32[]{:S(2)}) collective-permute-start(bf16[272,512]{1,0:T(8,128)(2,1)} %get-tuple-element.90), channel_id=1, source_target_pairs={{0,5},{1,6},{2,7},{3,0},{4,1},{5,2},{6,3},{7,4},{8,13},{9,14},{10,... | collective-permute-start | bytes 835592 | tf_op jit(solution)/shard_map/ppermute | solution.py:483
  135.3 13.1 %collective-permute-start.20 = (bf16[272,512]{1,0:T(8,128)(2,1)}, bf16[272,512]{1,0:T(8,128)(2,1)}, u32[]{:S(2)}, u32[]{:S(2)}) collective-permute-start(bf16[272,512]{1,0:T(8,128)(2,1)} %get-tuple-element.91), channel_id=1, source_target_pairs={{0,6},{1,7},{2,0},{3,1},{4,2},{5,3},{6,4},{7,5},{8,14},{9,15},{10,... | collective-permute-start | bytes 835592 | tf_op jit(solution)/shard_map/ppermute | solution.py:483
  136.0 19.7 %collective-permute-start.21 = (bf16[272,512]{1,0:T(8,128)(2,1)}, bf16[272,512]{1,0:T(8,128)(2,1)}, u32[]{:S(2)}, u32[]{:S(2)}) collective-permute-start(bf16[272,512]{1,0:T(8,128)(2,1)} %get-tuple-element.92), channel_id=1, source_target_pairs={{0,7},{1,0},{2,1},{3,2},{4,3},{5,4},{6,5},{7,6},{8,15},{9,8},{10,9... | collective-permute-start | bytes 835592 | tf_op jit(solution)/shard_map/ppermute | solution.py:483
  142.7 17.8 %copy-start.3 = (bf16[272,512]{1,0:T(8,128)(2,1)}, bf16[272,512]{1,0:T(8,128)(2,1)S(1)}, u32[]{:S(2)}) copy-start(bf16[272,512]{1,0:T(8,128)(2,1)S(1)} %collective-permute-done.17.refs_3_) | copy-start | bytes 835588
  142.7 29.8 %collective-permute-start.32 = (bf16[256,512]{1,0:T(8,128)(2,1)}, bf16[256,512]{1,0:T(8,128)(2,1)S(1)}, u32[]{:S(2)}, u32[]{:S(2)}) collective-permute-start(bf16[256,512]{1,0:T(8,128)(2,1)} %get-tuple-element.108), channel_id=1, source_target_pairs={{0,6},{1,7},{2,0},{3,1},{4,2},{5,3},{6,4},{7,5},{8,14},{9,15},{10,... | collective-permute-start | bytes 786440 | tf_op jit(solution)/shard_map/ppermute | solution.py:483
  146.1 28.1 %collective-permute-start.33 = (bf16[256,512]{1,0:T(8,128)(2,1)}, bf16[256,512]{1,0:T(8,128)(2,1)}, u32[]{:S(2)}, u32[]{:S(2)}) collective-permute-start(bf16[256,512]{1,0:T(8,128)(2,1)} %get-tuple-element.109), channel_id=1, source_target_pairs={{0,7},{1,0},{2,1},{3,2},{4,3},{5,4},{6,5},{7,6},{8,15},{9,8},{10,9... | collective-permute-start | bytes 786440 | tf_op jit(solution)/shard_map/ppermute | solution.py:483
  146.2 44.8 %collective-permute-start.37 = (bf16[256,512]{1,0:T(8,128)(2,1)}, bf16[256,512]{1,0:T(8,128)(2,1)S(1)}, u32[]{:S(2)}, u32[]{:S(2)}) collective-permute-start(bf16[256,512]{1,0:T(8,128)(2,1)} %get-tuple-element.113), channel_id=1, source_target_pairs={{0,1},{1,2},{2,3},{3,4},{4,5},{5,6},{6,7},{7,0},{8,9},{9,10},{10,1... | collective-permute-start | bytes 786440 | tf_op jit(solution)/shard_map/ppermute | solution.py:483
  148.5 44.5 %collective-permute-start.38 = (bf16[256,512]{1,0:T(8,128)(2,1)}, bf16[256,512]{1,0:T(8,128)(2,1)}, u32[]{:S(2)}, u32[]{:S(2)}) collective-permute-start(bf16[256,512]{1,0:T(8,128)(2,1)} %get-tuple-element.114), channel_id=1, source_target_pairs={{0,2},{1,3},{2,4},{3,5},{4,6},{5,7},{6,0},{7,1},{8,10},{9,11},{10,... | collective-permute-start | bytes 786440 | tf_op jit(solution)/shard_map/ppermute | solution.py:483
  155.7 38.6 %collective-permute-start.39 = (bf16[256,512]{1,0:T(8,128)(2,1)}, bf16[256,512]{1,0:T(8,128)(2,1)}, u32[]{:S(2)}, u32[]{:S(2)}) collective-permute-start(bf16[256,512]{1,0:T(8,128)(2,1)} %get-tuple-element.115), channel_id=1, source_target_pairs={{0,3},{1,4},{2,5},{3,6},{4,7},{5,0},{6,1},{7,2},{8,11},{9,12},{10,... | collective-permute-start | bytes 786440 | tf_op jit(solution)/shard_map/ppermute | solution.py:483
  159.9 19.2 %copy-start = (bf16[4,2560]{1,0:T(4,128)(2,1)}, bf16[4,2560]{1,0:T(4,128)(2,1)S(1)}, u32[]{:S(2)}) copy-start(bf16[4,2560]{1,0:T(4,128)(2,1)S(1)} %add_add_fusion.refs_7_) | copy-start | bytes 61444
  172.4 18.5 %copy-start.20 = (bf16[256,512]{1,0:T(8,128)(2,1)}, bf16[256,512]{1,0:T(8,128)(2,1)S(1)}, u32[]{:S(2)}) copy-start(bf16[256,512]{1,0:T(8,128)(2,1)S(1)} %collective-permute-done.32.refs_5_) | copy-start | bytes 786436
  172.4 3.3 collective-permute-start.22
  174.2 4.8 %collective-permute-start.23 = (bf16[16,128]{1,0:T(8,128)(2,1)}, bf16[16,128]{1,0:T(8,128)(2,1)S(1)}, u32[]{:S(2)}, u32[]{:S(2)}) collective-permute-start(bf16[16,128]{1,0:T(8,128)(2,1)} %get-tuple-element.95), channel_id=1, source_target_pairs={{0,16},{8,24},{1,17},{9,25},{2,18},{10,26},{3,19},{11,27},{4,20},{... | collective-permute-start | bytes 12296 | tf_op jit(solution)/shard_map/ppermute | solution.py:488
  175.7 19.9 %collective-permute-start.40 = (bf16[256,512]{1,0:T(8,128)(2,1)}, bf16[256,512]{1,0:T(8,128)(2,1)}, u32[]{:S(2)}, u32[]{:S(2)}) collective-permute-start(bf16[256,512]{1,0:T(8,128)(2,1)} %get-tuple-element.116), channel_id=1, source_target_pairs={{0,4},{1,5},{2,6},{3,7},{4,0},{5,1},{6,2},{7,3},{8,12},{9,13},{10,... | collective-permute-start | bytes 786440 | tf_op jit(solution)/shard_map/ppermute | solution.py:483
  179.0 17.3 %collective-permute-start.41 = (bf16[256,512]{1,0:T(8,128)(2,1)}, bf16[256,512]{1,0:T(8,128)(2,1)}, u32[]{:S(2)}, u32[]{:S(2)}) collective-permute-start(bf16[256,512]{1,0:T(8,128)(2,1)} %get-tuple-element.117), channel_id=1, source_target_pairs={{0,5},{1,6},{2,7},{3,0},{4,1},{5,2},{6,3},{7,4},{8,13},{9,14},{10,... | collective-permute-start | bytes 786440 | tf_op jit(solution)/shard_map/ppermute | solution.py:483
  191.7 10.5 %collective-permute-start.24 = (bf16[256,512]{1,0:T(8,128)(2,1)}, bf16[256,512]{1,0:T(8,128)(2,1)S(1)}, u32[]{:S(2)}, u32[]{:S(2)}) collective-permute-start(bf16[256,512]{1,0:T(8,128)(2,1)} %get-tuple-element.101), channel_id=1, source_target_pairs={{0,8},{8,16},{16,24},{1,9},{9,17},{17,25},{2,10},{10,18},{18,26},{... | collective-permute-start | bytes 786440 | tf_op jit(solution)/shard_map/ppermute | solution.py:488
  193.0 21.0 %collective-permute-start.25 = (bf16[256,512]{1,0:T(8,128)(2,1)}, bf16[256,512]{1,0:T(8,128)(2,1)S(1)}, u32[]{:S(2)}, u32[]{:S(2)}) collective-permute-start(bf16[256,512]{1,0:T(8,128)(2,1)} %get-tuple-element.101), channel_id=1, source_target_pairs={{0,16},{8,24},{1,17},{9,25},{2,18},{10,26},{3,19},{11,27},{4,20},{... | collective-permute-start | bytes 786440 | tf_op jit(solution)/shard_map/ppermute | solution.py:488
  194.3 20.5 %collective-permute-start.26 = (bf16[256,512]{1,0:T(8,128)(2,1)}, bf16[256,512]{1,0:T(8,128)(2,1)S(1)}, u32[]{:S(2)}, u32[]{:S(2)}) collective-permute-start(bf16[256,512]{1,0:T(8,128)(2,1)} %get-tuple-element.101), channel_id=1, source_target_pairs={{0,24},{1,25},{2,26},{3,27},{4,28},{5,29},{6,30},{7,31}} | collective-permute-start | bytes 786440 | tf_op jit(solution)/shard_map/ppermute | solution.py:488
  195.6 31.8 %collective-permute-start.42 = (bf16[256,512]{1,0:T(8,128)(2,1)}, bf16[256,512]{1,0:T(8,128)(2,1)}, u32[]{:S(2)}, u32[]{:S(2)}) collective-permute-start(bf16[256,512]{1,0:T(8,128)(2,1)} %get-tuple-element.118), channel_id=1, source_target_pairs={{0,6},{1,7},{2,0},{3,1},{4,2},{5,3},{6,4},{7,5},{8,14},{9,15},{10,... | collective-permute-start | bytes 786440 | tf_op jit(solution)/shard_map/ppermute | solution.py:483
  196.3 32.4 %collective-permute-start.43 = (bf16[256,512]{1,0:T(8,128)(2,1)}, bf16[256,512]{1,0:T(8,128)(2,1)}, u32[]{:S(2)}, u32[]{:S(2)}) collective-permute-start(bf16[256,512]{1,0:T(8,128)(2,1)} %get-tuple-element.119), channel_id=1, source_target_pairs={{0,7},{1,0},{2,1},{3,2},{4,3},{5,4},{6,5},{7,6},{8,15},{9,8},{10,9... | collective-permute-start | bytes 786440 | tf_op jit(solution)/shard_map/ppermute | solution.py:483
  202.2 39.2 %collective-permute-start.47 = (bf16[256,512]{1,0:T(8,128)(2,1)}, bf16[256,512]{1,0:T(8,128)(2,1)}, u32[]{:S(2)}, u32[]{:S(2)}) collective-permute-start(bf16[256,512]{1,0:T(8,128)(2,1)} %get-tuple-element.124), channel_id=1, source_target_pairs={{0,1},{1,2},{2,3},{3,4},{4,5},{5,6},{6,7},{7,0},{8,9},{9,10},{10,1... | collective-permute-start | bytes 786440 | tf_op jit(solution)/shard_map/ppermute | solution.py:483
  213.9 28.8 %collective-permute-start.48 = (bf16[256,512]{1,0:T(8,128)(2,1)}, bf16[256,512]{1,0:T(8,128)(2,1)}, u32[]{:S(2)}, u32[]{:S(2)}) collective-permute-start(bf16[256,512]{1,0:T(8,128)(2,1)} %get-tuple-element.125), channel_id=1, source_target_pairs={{0,2},{1,3},{2,4},{3,5},{4,6},{5,7},{6,0},{7,1},{8,10},{9,11},{10,... | collective-permute-start | bytes 786440 | tf_op jit(solution)/shard_map/ppermute | solution.py:483
  215.5 28.5 %collective-permute-start.34 = (bf16[256,512]{1,0:T(8,128)(2,1)}, bf16[256,512]{1,0:T(8,128)(2,1)S(1)}, u32[]{:S(2)}, u32[]{:S(2)}) collective-permute-start(bf16[256,512]{1,0:T(8,128)(2,1)} %get-tuple-element.111), channel_id=1, source_target_pairs={{0,8},{8,16},{16,24},{1,9},{9,17},{17,25},{2,10},{10,18},{18,26},{... | collective-permute-start | bytes 786440 | tf_op jit(solution)/shard_map/ppermute | solution.py:488
  227.4 17.9 %collective-permute-start.35 = (bf16[256,512]{1,0:T(8,128)(2,1)}, bf16[256,512]{1,0:T(8,128)(2,1)S(1)}, u32[]{:S(2)}, u32[]{:S(2)}) collective-permute-start(bf16[256,512]{1,0:T(8,128)(2,1)} %get-tuple-element.111), channel_id=1, source_target_pairs={{0,16},{8,24},{1,17},{9,25},{2,18},{10,26},{3,19},{11,27},{4,20},{... | collective-permute-start | bytes 786440 | tf_op jit(solution)/shard_map/ppermute | solution.py:488
  228.7 22.6 %collective-permute-start.36 = (bf16[256,512]{1,0:T(8,128)(2,1)}, bf16[256,512]{1,0:T(8,128)(2,1)S(1)}, u32[]{:S(2)}, u32[]{:S(2)}) collective-permute-start(bf16[256,512]{1,0:T(8,128)(2,1)} %get-tuple-element.111), channel_id=1, source_target_pairs={{0,24},{1,25},{2,26},{3,27},{4,28},{5,29},{6,30},{7,31}} | collective-permute-start | bytes 786440 | tf_op jit(solution)/shard_map/ppermute | solution.py:488
  241.4 10.0 %collective-permute-start.44 = (bf16[256,512]{1,0:T(8,128)(2,1)}, bf16[256,512]{1,0:T(8,128)(2,1)}, u32[]{:S(2)}, u32[]{:S(2)}) collective-permute-start(bf16[256,512]{1,0:T(8,128)(2,1)} %get-tuple-element.122), channel_id=1, source_target_pairs={{0,8},{8,16},{16,24},{1,9},{9,17},{17,25},{2,10},{10,18},{18,26},{... | collective-permute-start | bytes 786440 | tf_op jit(solution)/shard_map/ppermute | solution.py:488
  242.7 14.8 %collective-permute-start.45 = (bf16[256,512]{1,0:T(8,128)(2,1)}, bf16[256,512]{1,0:T(8,128)(2,1)}, u32[]{:S(2)}, u32[]{:S(2)}) collective-permute-start(bf16[256,512]{1,0:T(8,128)(2,1)} %get-tuple-element.122), channel_id=1, source_target_pairs={{0,16},{8,24},{1,17},{9,25},{2,18},{10,26},{3,19},{11,27},{4,20},{... | collective-permute-start | bytes 786440 | tf_op jit(solution)/shard_map/ppermute | solution.py:488
  244.0 17.7 %copy-start.4 = (bf16[256,512]{1,0:T(8,128)(2,1)}, bf16[256,512]{1,0:T(8,128)(2,1)S(1)}, u32[]{:S(2)}) copy-start(bf16[256,512]{1,0:T(8,128)(2,1)S(1)} %collective-permute-done.34.refs_8_) | copy-start | bytes 786436
  244.0 16.4 %collective-permute-start.46 = (bf16[256,512]{1,0:T(8,128)(2,1)}, bf16[256,512]{1,0:T(8,128)(2,1)}, u32[]{:S(2)}, u32[]{:S(2)}) collective-permute-start(bf16[256,512]{1,0:T(8,128)(2,1)} %get-tuple-element.122), channel_id=1, source_target_pairs={{0,24},{1,25},{2,26},{3,27},{4,28},{5,29},{6,30},{7,31}} | collective-permute-start | bytes 786440 | tf_op jit(solution)/shard_map/ppermute | solution.py:488
  245.3 16.4 %copy-start.5 = (bf16[256,512]{1,0:T(8,128)(2,1)}, bf16[256,512]{1,0:T(8,128)(2,1)S(1)}, u32[]{:S(2)}) copy-start(bf16[256,512]{1,0:T(8,128)(2,1)S(1)} %collective-permute-done.35.refs_9_) | copy-start | bytes 786436
  245.4 36.2 %collective-permute-start.49 = (bf16[256,512]{1,0:T(8,128)(2,1)}, bf16[256,512]{1,0:T(8,128)(2,1)}, u32[]{:S(2)}, u32[]{:S(2)}) collective-permute-start(bf16[256,512]{1,0:T(8,128)(2,1)} %get-tuple-element.126), channel_id=1, source_target_pairs={{0,3},{1,4},{2,5},{3,6},{4,7},{5,0},{6,1},{7,2},{8,11},{9,12},{10,... | collective-permute-start | bytes 786440 | tf_op jit(solution)/shard_map/ppermute | solution.py:483
  251.3 32.4 %collective-permute-start.50 = (bf16[256,512]{1,0:T(8,128)(2,1)}, bf16[256,512]{1,0:T(8,128)(2,1)}, u32[]{:S(2)}, u32[]{:S(2)}) collective-permute-start(bf16[256,512]{1,0:T(8,128)(2,1)} %get-tuple-element.127), channel_id=1, source_target_pairs={{0,4},{1,5},{2,6},{3,7},{4,0},{5,1},{6,2},{7,3},{8,12},{9,13},{10,... | collective-permute-start | bytes 786440 | tf_op jit(solution)/shard_map/ppermute | solution.py:483
  251.4 32.3 %collective-permute-start.51 = (bf16[256,512]{1,0:T(8,128)(2,1)}, bf16[256,512]{1,0:T(8,128)(2,1)}, u32[]{:S(2)}, u32[]{:S(2)}) collective-permute-start(bf16[256,512]{1,0:T(8,128)(2,1)} %get-tuple-element.128), channel_id=1, source_target_pairs={{0,5},{1,6},{2,7},{3,0},{4,1},{5,2},{6,3},{7,4},{8,13},{9,14},{10,... | collective-permute-start | bytes 786440 | tf_op jit(solution)/shard_map/ppermute | solution.py:483
  257.5 29.0 %collective-permute-start.52 = (bf16[256,512]{1,0:T(8,128)(2,1)}, bf16[256,512]{1,0:T(8,128)(2,1)}, u32[]{:S(2)}, u32[]{:S(2)}) collective-permute-start(bf16[256,512]{1,0:T(8,128)(2,1)} %get-tuple-element.129), channel_id=1, source_target_pairs={{0,6},{1,7},{2,0},{3,1},{4,2},{5,3},{6,4},{7,5},{8,14},{9,15},{10,... | collective-permute-start | bytes 786440 | tf_op jit(solution)/shard_map/ppermute | solution.py:483
  260.4 31.7 %collective-permute-start.53 = (bf16[256,512]{1,0:T(8,128)(2,1)}, bf16[256,512]{1,0:T(8,128)(2,1)}, u32[]{:S(2)}, u32[]{:S(2)}) collective-permute-start(bf16[256,512]{1,0:T(8,128)(2,1)} %get-tuple-element.130), channel_id=1, source_target_pairs={{0,7},{1,0},{2,1},{3,2},{4,3},{5,4},{6,5},{7,6},{8,15},{9,8},{10,9... | collective-permute-start | bytes 786440 | tf_op jit(solution)/shard_map/ppermute | solution.py:483
  303.4 3.9 %collective-permute-start.54 = (bf16[256,512]{1,0:T(8,128)(2,1)}, bf16[256,512]{1,0:T(8,128)(2,1)S(1)}, u32[]{:S(2)}, u32[]{:S(2)}) collective-permute-start(bf16[256,512]{1,0:T(8,128)(2,1)} %get-tuple-element.133), channel_id=1, source_target_pairs={{0,8},{8,16},{16,24},{1,9},{9,17},{17,25},{2,10},{10,18},{18,26},{... | collective-permute-start | bytes 786440 | tf_op jit(solution)/shard_map/ppermute | solution.py:488
  304.7 16.4 %collective-permute-start.55 = (bf16[256,512]{1,0:T(8,128)(2,1)}, bf16[256,512]{1,0:T(8,128)(2,1)S(1)}, u32[]{:S(2)}, u32[]{:S(2)}) collective-permute-start(bf16[256,512]{1,0:T(8,128)(2,1)} %get-tuple-element.133), channel_id=1, source_target_pairs={{0,16},{8,24},{1,17},{9,25},{2,18},{10,26},{3,19},{11,27},{4,20},{... | collective-permute-start | bytes 786440 | tf_op jit(solution)/shard_map/ppermute | solution.py:488
  306.0 17.1 %collective-permute-start.56 = (bf16[256,512]{1,0:T(8,128)(2,1)}, bf16[256,512]{1,0:T(8,128)(2,1)S(1)}, u32[]{:S(2)}, u32[]{:S(2)}) collective-permute-start(bf16[256,512]{1,0:T(8,128)(2,1)} %get-tuple-element.133), channel_id=1, source_target_pairs={{0,24},{1,25},{2,26},{3,27},{4,28},{5,29},{6,30},{7,31}} | collective-permute-start | bytes 786440 | tf_op jit(solution)/shard_map/ppermute | solution.py:488
  307.4 15.8 %copy-start.7 = (bf16[256,512]{1,0:T(8,128)(2,1)}, bf16[256,512]{1,0:T(8,128)(2,1)S(1)}, u32[]{:S(2)}) copy-start(bf16[256,512]{1,0:T(8,128)(2,1)S(1)} %collective-permute-done.54.refs_8_) | copy-start | bytes 786436
  (19 other events, 95.6 us)
where the time goes:
time: 336 us; the launch traced here: 334 us
  waiting for transfers between devices  132 us (39%)
  Pallas kernels  117 us (35%)
  starting transfers between devices  76.8 us (23%)
  local copies, waits for them, and re-layouts  6.91 us (2%)
    ppermute x35, waiting for transfers between devices, rotate(): lax.ppermute(arrays[s - 1], 'inner', [(i, (i + s) % n) for i in range(n)])  86.7 us
    ppermute x35, starting transfers between devices, rotate(): lax.ppermute(arrays[s - 1], 'inner', [(i, (i + s) % n) for i in range(n)])  52.8 us
    pallas_call x4, Pallas kernels, convolve(): pl.pallas_call(body, grid_spec=pltpu.PrefetchScalarGridSpec(num_scalar_pr...  45.3 us
    pallas_call x4, Pallas kernels, emit(): pl.pallas_call(body, grid=(total // tok,), in_specs=[ANY] * len(alias) +...  39.5 us
    ppermute x14, waiting for transfers between devices, forward(): return lax.ppermute(a, 'slab', [(i, i + by) for i in range(n_slab - by)])  23.7 us
    ppermute x8, waiting for transfers between devices, shards(): lax.ppermute(e, ('slab', 'inner'), [(s * n + n - 1, (s + 1) * n + j) for...  21.4 us
    ppermute x14, starting transfers between devices, forward(): return lax.ppermute(a, 'slab', [(i, i + by) for i in range(n_slab - by)])  18.1 us
    pallas_call x4, Pallas kernels, pack_x(): pl.pallas_call(body, grid_spec=pltpu.PrefetchScalarGridSpec(num_scalar_pr...  15.1 us
  transfers between devices with their start and end apart: 57, of which 16 were waited for; matrix products, arithmetic and copies ran while one was open for 1% of the time, Pallas kernels for 27%

commit v1 on v0

v1 whole, which is shorter than its diff:
```python
import jax
import jax.numpy as jnp
from jax import lax
from jax.experimental import pallas as pl
from jax.experimental.pallas import tpu as pltpu
from jax.sharding import PartitionSpec as P


HEADS = 256
HEADDIM = 64
STATE = 256
GROUPS = 8
CONV = 4
LANES = 128
EDGE_ROWS = 8
SENT_ROWS = 4
SEG = 16


F32 = jnp.float32
BF16 = jnp.bfloat16
ANY = pl.BlockSpec(memory_space=pl.ANY)


def whole(shape):
    return pl.BlockSpec(shape, lambda *_: (0,) * len(shape))


def params():
    return pltpu.CompilerParams(vmem_limit_bytes=63 << 20)


def cost(flops, moved):
    return pl.CostEstimate(flops=flops, bytes_accessed=moved, transcendentals=0)


def chunk_widths(channels):
    return [channels // 4] * 4


def rows_ahead(edge_ref):
    e = edge_ref[...].astype(F32)
    return jnp.concatenate([jnp.zeros((EDGE_ROWS - SENT_ROWS, e.shape[1]), F32), e], axis=0)


def silu(x):
    half = 0.5 * x
    return half + half * jnp.tanh(half)


def conv_rows(carry, rows, weight, bias):
    ext = jnp.concatenate([carry, rows], axis=0)
    acc = bias + weight[CONV - 1 : CONV] * rows
    for back in range(1, CONV):
        shifted = pltpu.roll(ext, back, 0)[EDGE_ROWS:]
        acc = acc + weight[CONV - 1 - back : CONV - back] * shifted
    return silu(acc).astype(BF16)


def spread(per_head, first, width):
    lane = lax.broadcasted_iota(jnp.int32, per_head.shape, 1)
    parts = []
    for h in range(first, first + width // HEADDIM, LANES // HEADDIM):
        parts.append(jnp.take_along_axis(per_head, h + lane // HEADDIM, axis=1))
    return parts[0] if len(parts) == 1 else jnp.concatenate(parts, axis=1)


def pack_bc(bc_in, dt_raw, n, heads_dev, per_group):
    tok = bc_in.shape[0]

    def body(bc_ref, dt_ref, out_ref):
        turned = dt_ref[...].astype(F32).T.astype(BF16)
        for d in range(n):
            g = d * heads_dev // per_group * STATE
            out_ref[d, :tok, :STATE] = bc_ref[:, g : g + STATE]
            g += GROUPS * STATE
            out_ref[d, :tok, STATE:] = bc_ref[:, g : g + STATE]
            for seg in range(2):
                first = d * heads_dev + seg * SEG
                if seg * SEG < heads_dev:
                    part = turned[first : first + SEG]
                else:
                    part = jnp.zeros((SEG, tok), BF16)
                out_ref[d, tok:, seg * tok : (seg + 1) * tok] = part

    shape = (n, tok + SEG, 2 * STATE)
    return pl.pallas_call(
        body,
        grid=(1,),
        in_specs=[whole(bc_in.shape), whole(dt_raw.shape)],
        out_specs=whole(shape),
        out_shape=jax.ShapeDtypeStruct(shape, BF16),
        compiler_params=params(),
        cost_estimate=cost(0, 4 * bc_in.size),
        name="pack_bc",
    )(bc_in, dt_raw)


def by_permutes(k):
    return k % 2 == 0


def pack_x(me, x_in, n, channels, widths):
    tok = x_in.shape[0]
    step = min(64, tok)
    specs, shapes = [], []
    for k, width in enumerate(widths):
        if by_permutes(k):
            specs += [pl.BlockSpec((step, width), lambda i, me: (i, 0))] * (n - 1)
            shapes += [(tok, width)] * (n - 1)
        else:
            specs.append(pl.BlockSpec((n, step, width), lambda i, me: (0, i, 0)))
            shapes.append((n, tok, width))

    def body(me_ref, x_ref, *outs):
        outs, first = list(outs), 0
        for k, width in enumerate(widths):
            if by_permutes(k):
                for s in range(1, n):
                    col = ((me_ref[0] + s) % n) * channels + first
                    outs.pop(0)[...] = x_ref[:, pl.ds(pl.multiple_of(col, LANES), width)]
            else:
                out = outs.pop(0)
                for d in range(n):
                    col = d * channels + first
                    out[d] = x_ref[:, col : col + width]
            first += width

    parts = pl.pallas_call(
        body,
        grid_spec=pltpu.PrefetchScalarGridSpec(
            num_scalar_prefetch=1,
            grid=(tok // step,),
            in_specs=[pl.BlockSpec((step, n * channels), lambda i, me: (i, 0))],
            out_specs=specs,
        ),
        out_shape=[jax.ShapeDtypeStruct(shape, BF16) for shape in shapes],
        compiler_params=params(),
        cost_estimate=cost(0, 4 * tok * channels * n),
        name="pack_x",
    )(me, x_in)
    parts, sets = list(parts), []
    for k in range(len(widths)):
        count = n - 1 if by_permutes(k) else 1
        sets.append([parts.pop(0) for _ in range(count)])
    return sets


def pack_edge(x_in, bc_in, n, channels, heads_dev, per_group):
    tok = x_in.shape[0]
    wide = channels + 2 * STATE

    def body(x_ref, bc_ref, *outs):
        x = x_ref[...].astype(F32)[2 * EDGE_ROWS - SENT_ROWS :].astype(BF16)
        bc = bc_ref[...].astype(F32)[2 * EDGE_ROWS - SENT_ROWS :].astype(BF16)
        for j in range(n):
            g = j * heads_dev // per_group
            outs[j][:, :channels] = x[:, j * channels : (j + 1) * channels]
            outs[j][:, channels : channels + STATE] = bc[:, g * STATE : (g + 1) * STATE]
            g += GROUPS
            outs[j][:, channels + STATE :] = bc[:, g * STATE : (g + 1) * STATE]

    last = tok // (2 * EDGE_ROWS) - 1
    return pl.pallas_call(
        body,
        grid=(1,),
        in_specs=[
            pl.BlockSpec((2 * EDGE_ROWS, x_in.shape[1]), lambda i: (last, 0)),
            pl.BlockSpec((2 * EDGE_ROWS, bc_in.shape[1]), lambda i: (last, 0)),
        ],
        out_specs=[whole((SENT_ROWS, wide))] * n,
        out_shape=[jax.ShapeDtypeStruct((SENT_ROWS, wide), BF16)] * n,
        compiler_params=params(),
        cost_estimate=cost(0, 4 * EDGE_ROWS * wide * n),
        name="pack_edge",
    )(x_in, bc_in)


def prepare(me, message, edge, weight, bias, dt_bias, a_log, n, heads_dev, per_group):
    rows = message.shape[1]
    tok = rows - SEG
    total = n * tok

    def body(me_ref, *refs):
        msg_ref, refs = refs[0], refs[1:]
        edge_ref, wb_ref, wc_ref, bb_ref, bc_ref, dtb_ref, al_ref = refs[:7]
        bt_out, c_out, m_out, wu_out, ec_out, dj_out, pj_out, dv_out = refs[7:15]
        buf, sems = refs[15:]
        copy = pltpu.make_async_copy(msg_ref, buf, sems.at[0])
        copy.start()
        copy.wait()

        def turn(w):
            pad = jnp.zeros((LANES - heads_dev, w.shape[1]), F32)
            return jnp.concatenate([w, pad], axis=0).T

        at = lax.broadcasted_iota(jnp.int32, (tok, tok), 0)
        to = lax.broadcasted_iota(jnp.int32, (tok, tok), 1)
        upto = jnp.where(at <= to, 1.0, 0.0).astype(F32)
        rate = -jnp.exp(al_ref[...])
        ends, aheads = [], [jnp.zeros((heads_dev, 1), F32)]
        for j in range(n):
            dt_raw = buf[j, tok:, :].astype(F32)
            segs = [dt_raw[:, i * tok : (i + 1) * tok] for i in range(heads_dev // SEG)]
            dt = jax.nn.softplus(jnp.concatenate(segs, axis=0) + dtb_ref[...])
            cum = jnp.dot(
                dt * rate,
                upto,
                precision=lax.Precision.HIGHEST,
                preferred_element_type=F32,
            )
            here = pl.ds(j * tok, tok)
            wu_out[here, :] = turn(dt * jnp.exp(-cum))
            ec_out[here, :] = turn(jnp.exp(cum))
            ends.append(cum[:, tok - 1 :])
            aheads.append(aheads[-1] + ends[-1])
        pad = jnp.zeros((heads_dev, LANES - n), F32)
        dj_out[...] = turn(jnp.exp(jnp.concatenate(ends + [pad], axis=1)))
        pj_out[...] = turn(jnp.exp(jnp.concatenate(aheads[:-1] + [pad], axis=1)))
        decay = jnp.broadcast_to(jnp.exp(aheads[-1]), (heads_dev, LANES))
        dv_out[...] = turn(decay)[: dv_out.shape[0]]

        strip = 32
        lower = at >= to

        def block(j, carry):
            def step(i, carry):
                r = pl.multiple_of(i * strip, strip)
                x = buf[j, pl.ds(r, strip), :].astype(F32)
                new = []
                for half, w_ref, b_ref in ((0, wb_ref, bb_ref), (1, wc_ref, bc_ref)):
                    mine = x[:, half * STATE : (half + 1) * STATE]
                    done = conv_rows(carry[half], mine, w_ref[...], b_ref[...])
                    buf[j, pl.ds(r, strip), half * STATE : (half + 1) * STATE] = done
                    new.append(mine[strip - EDGE_ROWS :])
                return tuple(new)

            carry = lax.fori_loop(0, tok // strip, step, carry)
            b, c = buf[j, :tok, :STATE], buf[j, :tok, STATE:]
            t = pl.multiple_of(j * tok, tok)
            turned = b.astype(F32).T.astype(BF16)
            bt_out[:, pl.ds(t, tok)] = turned
            c_out[pl.ds(t, tok), :] = c
            scores = jnp.dot(c, turned, preferred_element_type=F32)
            m_out[pl.ds(t, tok), :] = jnp.where(lower, scores, 0.0).astype(BF16)
            return carry

        e = rows_ahead(edge_ref)
        lax.fori_loop(0, n, block, (e[:, :STATE], e[:, STATE:]))

    def group(base):
        return lambda i, me: (0, base + me[0] * heads_dev // per_group)

    vec = (heads_dev, 1)
    shapes = [(STATE, total), (total, STATE), (total, tok)]
    wide = [(total, LANES), (total, LANES), (LANES, LANES), (LANES, LANES), (EDGE_ROWS, LANES)]
    return pl.pallas_call(
        body,
        grid_spec=pltpu.PrefetchScalarGridSpec(
            num_scalar_prefetch=1,
            grid=(1,),
            in_specs=[ANY]
            + [
                whole(edge.shape),
                pl.BlockSpec((CONV, STATE), group(0)),
                pl.BlockSpec((CONV, STATE), group(GROUPS)),
                pl.BlockSpec((1, STATE), group(0)),
                pl.BlockSpec((1, STATE), group(GROUPS)),
                whole(vec),
                whole(vec),
            ],
            out_specs=[whole(s) for s in shapes + wide],
            scratch_shapes=[
                pltpu.VMEM((n, rows, 2 * STATE), BF16),
                pltpu.SemaphoreType.DMA((1,)),
            ],
        ),
        out_shape=[jax.ShapeDtypeStruct(s, BF16) for s in shapes]
        + [jax.ShapeDtypeStruct(s, F32) for s in wide],
        compiler_params=params(),
        cost_estimate=cost(4 * total * STATE * tok, 20 * total * STATE),
        name="prepare",
    )(me, message, edge, weight, weight, bias, bias, dt_bias, a_log)


def convolve(me, x_in, received, edge, weight, bias, bt, wu, dj, n, channels, width, first, after):
    tok = x_in.shape[0]
    total = n * tok
    got_count = len(received)
    group = min(width, 256)
    strip = 64
    lead = 2 * EDGE_ROWS

    def body(me_ref, x_ref, *refs):
        got, refs = refs[:got_count], refs[got_count:]
        edge_ref, w_ref, b_ref, bt_ref, wu_ref, dj_ref = refs[:6]
        xc_ref, u_ref, s_ref, end_out = refs[6 + len(after) : 10 + len(after)]
        x_buf, xf_buf, xc_buf, u_buf, s_buf, state, decs, sems, out_sems = refs[
            10 + len(after) :
        ]

        def slot(j):
            return x_buf.at[pl.ds(pl.multiple_of(j * tok, tok), tok), :]

        for s in range(n):
            if got_count == 1:
                j, src = s, got[0].at[s]
            else:
                j = lax.rem(me_ref[0] - s + n, n)
                if s:
                    src = got[s - 1]
                else:
                    col = pl.multiple_of(me_ref[0] * channels + first, LANES)
                    src = x_ref.at[:, pl.ds(col, width)]
            pltpu.make_async_copy(src, slot(j), sems.at[j]).start()
        decs[...] = spread(dj_ref[: decs.shape[0], :], first // HEADDIM, width)
        e = rows_ahead(edge_ref)
        for g in range(width // LANES):
            xf_buf[g, EDGE_ROWS:lead, :] = e[:, g * LANES : (g + 1) * LANES]
        state[...] = jnp.zeros_like(state)

        def outgoing(j):
            t = pl.multiple_of(j * tok, tok)
            q = pl.multiple_of(j * STATE, STATE)
            return (
                pltpu.make_async_copy(
                    xc_buf.at[pl.ds(t, tok), :], xc_ref.at[pl.ds(t, tok), :], out_sems.at[0, j]
                ),
                pltpu.make_async_copy(
                    u_buf.at[pl.ds(t, tok), :], u_ref.at[pl.ds(t, tok), :], out_sems.at[1, j]
                ),
                pltpu.make_async_copy(
                    s_buf.at[pl.ds(q, STATE), :], s_ref.at[pl.ds(q, STATE), :], out_sems.at[2, j]
                ),
            )

        def block(j, carry):
            pltpu.make_async_copy(slot(j), slot(j), sems.at[j]).wait()
            t = pl.multiple_of(j * tok, tok)
            q = pl.multiple_of(j * STATE, STATE)
            for i in range(tok // strip):
                r = pl.multiple_of(t + i * strip, strip)
                per_head = wu_ref[pl.ds(r, strip), :]
                for g in range(width // LANES):
                    cols = slice(g * LANES, (g + 1) * LANES)
                    low = lead + i * strip
                    x = x_buf[pl.ds(r, strip), cols].astype(F32)
                    xf_buf[g, low : low + strip, :] = x
                    acc = b_ref[:, cols] + w_ref[CONV - 1 :, cols] * x
                    for back in range(1, CONV):
                        acc = acc + (
                            w_ref[CONV - 1 - back : CONV - back, cols]
                            * xf_buf[g, low - back : low - back + strip, :]
                        )
                    xc = silu(acc).astype(BF16)
                    xc_buf[pl.ds(r, strip), cols] = xc
                    scale = spread(per_head, (first + g * LANES) // HEADDIM, LANES)
                    u_buf[pl.ds(r, strip), cols] = (xc.astype(F32) * scale).astype(BF16)
            for g in range(width // LANES):
                xf_buf[g, EDGE_ROWS:lead, :] = xf_buf[g, lead + tok - EDGE_ROWS : lead + tok, :]
            lhs = bt_ref[:, pl.ds(t, tok)]
            for g in range(width // group):
                cols = slice(g * group, (g + 1) * group)
                old = state[:, cols]
                s_buf[pl.ds(q, STATE), cols] = old.astype(BF16)
                added = jnp.dot(lhs, u_buf[pl.ds(t, tok), cols], preferred_element_type=F32)
                state[:, cols] = decs[pl.ds(j, 1), cols] * (old + added)
            for copy in outgoing(j):
                copy.start()
            return carry

        lax.fori_loop(0, n, block, 0)
        end_out[...] = state[...].astype(BF16)
        for j in range(n):
            for copy in outgoing(j):
                copy.wait()

    def columns(rows):
        per = channels // width if channels % width == 0 and first % width == 0 else 0
        if per:
            return pl.BlockSpec((rows, width), lambda i, me: (0, me[0] * per + first // width))
        return pl.BlockSpec(
            (pl.Element(rows), pl.Element(width)),
            lambda i, me: (0, pl.multiple_of(me[0] * channels + first, LANES)),
        )

    return pl.pallas_call(
        body,
        grid_spec=pltpu.PrefetchScalarGridSpec(
            num_scalar_prefetch=1,
            grid=(1,),
            in_specs=[ANY] * (1 + got_count)
            + [
                whole((SENT_ROWS, width)),
                columns(CONV),
                columns(1),
                whole(bt.shape),
                whole(wu.shape),
                whole(dj.shape),
            ]
            + [ANY] * len(after),
            out_specs=[ANY, ANY, ANY, whole((STATE, width))],
            scratch_shapes=[
                pltpu.VMEM((total, width), BF16),
                pltpu.VMEM((width // LANES, lead + tok, LANES), F32),
                pltpu.VMEM((total, width), BF16),
                pltpu.VMEM((total, width), BF16),
                pltpu.VMEM((n * STATE, width), BF16),
                pltpu.VMEM((STATE, width), F32),
                pltpu.VMEM((-(-n // EDGE_ROWS) * EDGE_ROWS, width), F32),
                pltpu.SemaphoreType.DMA((n,)),
                pltpu.SemaphoreType.DMA((3, n)),
            ],
        ),
        out_shape=[
            jax.ShapeDtypeStruct((total, width), BF16),
            jax.ShapeDtypeStruct((total, width), BF16),
            jax.ShapeDtypeStruct((n * STATE, width), BF16),
            jax.ShapeDtypeStruct((STATE, width), BF16),
        ],
        compiler_params=params(),
        cost_estimate=cost(2 * total * STATE * width, 6 * total * width + 4 * total * STATE),
        name="convolve",
    )(me, x_in, *received, edge, weight, bias, bt, wu, dj, *after)


def emit(y, xc, u, s_loc, c, m, ec, pj, ends, decays, skip, channels, width, first):
    total = xc.shape[0]
    tok = m.shape[1]
    group = min(width, 256)
    n_ends, n_decays = len(ends), len(decays)
    alias = [] if y is None else [y]
    fold = 2

    def body(*refs):
        refs = refs[len(alias) :]
        xc_ref, u_ref, s_ref, c_ref, m_ref, ec_ref, pj_ref, skip_ref = refs[:8]
        end_refs, refs = refs[8 : 8 + n_ends], refs[8 + n_ends :]
        decay_refs, (out_ref, token_ref, carry, steps) = refs[:n_decays], refs[n_decays:]

        @pl.when(pl.program_id(0) == 0)
        def _():
            steps[...] = spread(pj_ref[: steps.shape[0], :], first // HEADDIM, width)
            carried = end_refs[-1][...].astype(F32)
            for i in reversed(range(n_ends - 1)):
                d = spread(decay_refs[i][...], first // HEADDIM, width)[:1]
                carried = end_refs[i][...].astype(F32) + d * carried
            carry[...] = carried
            token_ref[...] = jnp.zeros_like(token_ref)

        for b in range(fold):
            step = steps[pl.ds(pl.program_id(0) * fold + b, 1), :]
            rows = slice(b * tok, (b + 1) * tok)
            states = slice(b * STATE, (b + 1) * STATE)
            for g in range(width // group):
                cols = slice(g * group, (g + 1) * group)
                s = s_ref[states, cols].astype(F32) + step[:, cols] * carry[:, cols]
                acc = jnp.dot(m_ref[rows, :], u_ref[rows, cols], preferred_element_type=F32)
                acc += jnp.dot(c_ref[rows, :], s.astype(BF16), preferred_element_type=F32)
                e = spread(ec_ref[rows, :], (first + g * group) // HEADDIM, group)
                x = xc_ref[rows, cols].astype(F32)
                out_ref[rows, cols] = (e * acc + skip_ref[:, cols] * x).astype(BF16)

    def ahead(shape):
        return pl.BlockSpec((fold * shape[0], shape[1]), lambda j: (j, 0))

    if channels % width == 0 and first % width == 0:
        out_spec = pl.BlockSpec((fold * tok, width), lambda j: (j, first // width))
    else:
        out_spec = pl.BlockSpec(
            (pl.Element(fold * tok), pl.Element(width)), lambda j: (j * fold * tok, first)
        )
    return pl.pallas_call(
        body,
        grid=(total // (fold * tok),),
        in_specs=[ANY] * len(alias)
        + [
            ahead((tok, width)),
            ahead((tok, width)),
            ahead((STATE, width)),
            ahead((tok, STATE)),
            ahead((tok, tok)),
            ahead((tok, LANES)),
            whole(pj.shape),
            whole((1, width)),
        ]
        + [whole((STATE, width))] * n_ends
        + [whole((EDGE_ROWS, LANES))] * n_decays,
        out_specs=[out_spec, whole((EDGE_ROWS, LANES))],
        out_shape=[
            jax.ShapeDtypeStruct((total, channels), BF16),
            jax.ShapeDtypeStruct((EDGE_ROWS, LANES), F32),
        ],
        scratch_shapes=[
            pltpu.VMEM((STATE, width), F32),
            pltpu.VMEM((-(-total // tok // EDGE_ROWS) * EDGE_ROWS, width), F32),
        ],
        input_output_aliases={0: 0} if alias else {},
        compiler_params=params(),
        cost_estimate=cost(6 * total * STATE * width, 8 * total * width + 6 * total * STATE),
        name="emit",
    )(*alias, xc, u, s_loc, c, m, ec, pj, skip, *ends, *decays)


def shards(
    x_in,
    bc_in,
    dt_raw,
    dt_bias,
    a_log,
    d_skip,
    conv_x_weight,
    conv_x_bias,
    conv_bc_weight,
    conv_bc_bias,
):
    n = lax.axis_size("inner")
    n_slab = lax.axis_size("slab")
    heads_dev = HEADS // n
    channels = heads_dev * HEADDIM
    per_group = HEADS // GROUPS
    index = lax.axis_index("inner")
    me = index.astype(jnp.int32).reshape(1)

    middle = n // 2
    shifts = sorted(range(1, n), key=lambda s: abs(s - middle))

    def rotate(arrays, chosen):
        for s in chosen:
            arrays[s - 1] = lax.ppermute(
                arrays[s - 1], "inner", [(i, (i + s) % n) for i in range(n)]
            )

    def forward(a, by):
        return lax.ppermute(a, "slab", [(i, i + by) for i in range(n_slab - by)])

    def mine(v):
        return lax.dynamic_slice_in_dim(v, index * heads_dev, heads_dev, 0)

    def exchange(a):
        return lax.all_to_all(a, "inner", split_axis=0, concat_axis=0, tiled=True)

    def send(k, parts):
        if not by_permutes(k):
            return [exchange(parts[0])]
        rotate(parts, shifts)
        return parts

    widths = chunk_widths(channels)
    packed = pack_bc(bc_in, dt_raw, n, heads_dev, per_group)
    message = exchange(packed)
    packed_x = pack_x(me, x_in, n, channels, widths)
    received = [send(k, parts) for k, parts in enumerate(packed_x)]
    edges = pack_edge(x_in, bc_in, n, channels, heads_dev, per_group)
    edges = [
        lax.ppermute(
            e, ("slab", "inner"), [(s * n + n - 1, (s + 1) * n + j) for s in range(n_slab - 1)]
        )
        for j, e in enumerate(edges)
    ]
    edge = sum(edges)
    skip = jnp.repeat(mine(d_skip), HEADDIM)[None, :]
    bt, c, m, wu, ec, dj, pj, dv = prepare(
        me,
        message,
        edge[:, channels:],
        conv_bc_weight,
        conv_bc_bias[None, :],
        mine(dt_bias)[:, None],
        mine(a_log)[:, None],
        n,
        heads_dev,
        per_group,
    )
    decays = [forward(dv, by) for by in range(1, n_slab - 1)]
    y = None
    tokens, pending = [], []

    def finish():
        k, xc, u, s_loc, ends = pending.pop(0)
        cut = slice(sum(widths[:k]), sum(widths[: k + 1]))
        return emit(
            y,
            xc,
            u,
            s_loc,
            c,
            m,
            ec,
            pj,
            ends,
            decays,
            skip[:, cut],
            channels,
            widths[k],
            cut.start,
        )

    last = len(widths) - 1
    for k, width in enumerate(widths):
        first = sum(widths[:k])
        xc, u, s_loc, end = convolve(
            me,
            x_in,
            received[k],
            edge[:, first : first + width],
            conv_x_weight,
            conv_x_bias[None, :],
            bt,
            wu,
            dj,
            n,
            channels,
            width,
            first,
            decays if k == 0 else tokens[-1:],
        )
        ends = [forward(end, by) for by in range(1, n_slab)]
        pending.append((k, xc, u, s_loc, ends))
        while pending and (len(pending) > 1 or k >= last - 1):
            y, token = finish()
            tokens.append(token)
    return y


def solution(mesh):
    tokens = P(("slab", "inner"), None)
    placed = (tokens, tokens, tokens) + (P(),) * 7

    return jax.shard_map(
        shards, mesh=mesh, in_specs=placed, out_specs=P("slab", "inner"), check_vma=False
    )
```

time: 336 us -> 348 us (1.036)
  the two profiles are of different devices: /device:TPU:15 before, /device:TPU:0 now
where the time goes in v1:
time: 348 us; the launch traced here: 347 us
  starting transfers between devices  120 us (34%)
  Pallas kernels  88.7 us (25%)
  waiting for transfers between devices  76.5 us (22%)
  blocking collectives  55.3 us (16%)
  local copies, waits for them, and re-layouts  5.17 us (1%)
    ppermute x14, starting transfers between devices, rotate(): lax.ppermute(arrays[s - 1], 'inner', [(i, (i + s) % n) for i in range(n)])  76.6 us
    all_to_all x1, blocking collectives, exchange(): return lax.all_to_all(a, 'inner', split_axis=0, concat_axis=0, tiled=True)  55.3 us
    all_to_all x2, waiting for transfers between devices, exchange(): return lax.all_to_all(a, 'inner', split_axis=0, concat_axis=0, tiled=True)  45.2 us
    pallas_call x4, Pallas kernels, convolve(): pl.pallas_call(body, grid_spec=pltpu.PrefetchScalarGridSpec(num_scalar_pr...  37.1 us
    pallas_call x4, Pallas kernels, emit(): pl.pallas_call(body, grid=(total // (fold * tok),), in_specs=[ANY] * len(...  27.7 us
    ppermute x14, starting transfers between devices, forward(): return lax.ppermute(a, 'slab', [(i, i + by) for i in range(n_slab - by)])  26.8 us
    ppermute x14, waiting for transfers between devices, rotate(): lax.ppermute(arrays[s - 1], 'inner', [(i, (i + s) % n) for i in range(n)])  24.1 us
    pallas_call x1, Pallas kernels, prepare(): pl.pallas_call(body, grid_spec=pltpu.PrefetchScalarGridSpec(num_scalar_pr...  12.2 us
  transfers between devices with their start and end apart: 38, of which 5 were waited for; matrix products, arithmetic and copies ran while one was open for 1% of the time, Pallas kernels for 19%

profile of v1, /device:TPU:0, one launch (start us, length us, event | category | flops | bytes accessed | tf_op | source)
XLA Modules:
  0.0 346.6 jit_solution(539237904247010620)
XLA Ops:
  0.0 6.8 %pack_x.1 = (bf16[256,512]{1,0:T(8,128)(2,1)}, bf16[256,512]{1,0:T(8,128)(2,1)}, bf16[256,512]{1,0:T(8,128)(2,1)}, bf16[256,512]{1,0:T(8,128)(2,1)}, bf16[256,51...) custom-call(s32[1]{0:T(128)} %bitcast.me_ref, ...), custom_call_target="tpu_custom_call" | custom-call | bytes 16777216 | tf_op jit(solution)/shard_map/pack_x/pallas_call | solution.py:129
  6.8 7.3 %all-to-all-start.1 = ((bf16[8,256,512]{2,1,0:T(8,128)(2,1)}), bf16[8,256,512]{2,1,0:T(8,128)(2,1)}, u32[]{:S(2)}, u32[]{:S(2)}) async-start(bf16[8,256,512]{2,1,0:T(8,128)(2,1)} %get-tuple-element.87), calls=%async_computation.1 | async-start | bytes 4194304 | tf_op jit(solution)/shard_map/all_to_all | solution.py:541
  14.1 3.2 pack_bc.1
  17.3 45.2 %all-to-all-done.1.refs_0_ = bf16[8,256,512]{2,1,0:T(8,128)(2,1)} async-done(((bf16[8,256,512]{2,1,0:T(8,128)(2,1)}), bf16[8,256,512]{2,1,0:T(8,128)(2,1)}, u32[]{:S(2)}, u32[]{:S(2)}) %all-to-all-start.1) | async-done | bytes 2097184 | tf_op jit(solution)/shard_map/all_to_all | solution.py:541
  62.5 55.3 %all_to_all.15.refs_0_ = bf16[8,272,512]{2,1,0:T(8,128)(2,1)} all-to-all(bf16[8,272,512]{2,1,0:T(8,128)(2,1)} %pack_bc.1), channel_id=1, replica_groups=mesh['slab'=4,'inner'=8] {'inner'}, dimensions={0} | all-to-all | bytes 4456448 | tf_op jit(solution)/shard_map/all_to_all | solution.py:541
  117.8 4.4 %all-to-all-start.2 = ((bf16[8,256,512]{2,1,0:T(8,128)(2,1)}), bf16[8,256,512]{2,1,0:T(8,128)(2,1)}, u32[]{:S(2)}, u32[]{:S(2)}) async-start(bf16[8,256,512]{2,1,0:T(8,128)(2,1)} %get-tuple-element.106), calls=%async_computation.2 | async-start | bytes 4194304 | tf_op jit(solution)/shard_map/all_to_all | solution.py:541
  122.2 1.7 pack_edge.1
  123.9 0.7 collective-permute-start.7
  124.6 0.7 collective-permute-start.8
  125.3 0.7 collective-permute-start.9
  125.9 0.7 collective-permute-start.10
  126.6 0.7 collective-permute-start.11
  127.3 0.7 collective-permute-start.12
  128.0 0.7 collective-permute-start.13
  128.7 0.7 collective-permute-start.14
  129.3 0.1 dynamic-slice_bitcast_fusion
  129.4 0.7 copy.15.refs_7_
  130.1 0.7 copy.14.refs_6_
  130.8 1.9 collective-permute-start
  132.7 1.5 collective-permute-start.1
  134.2 2.4 collective-permute-start.2
  136.6 30.9 %collective-permute-start.3 = (bf16[256,512]{1,0:T(8,128)(2,1)}, bf16[256,512]{1,0:T(8,128)(2,1)S(1)}, u32[]{:S(2)}, u32[]{:S(2)}) collective-permute-start(bf16[256,512]{1,0:T(8,128)(2,1)} %get-tuple-element.62), channel_id=1, source_target_pairs={{0,4},{1,5},{2,6},{3,7},{4,0},{5,1},{6,2},{7,3},{8,12},{9,13},{10,... | collective-permute-start | bytes 786440 | tf_op jit(solution)/shard_map/ppermute | solution.py:530
  167.5 3.8 %collective-permute-start.4 = (bf16[256,512]{1,0:T(8,128)(2,1)}, bf16[256,512]{1,0:T(8,128)(2,1)S(1)}, u32[]{:S(2)}, u32[]{:S(2)}) collective-permute-start(bf16[256,512]{1,0:T(8,128)(2,1)} %get-tuple-element.63), channel_id=1, source_target_pairs={{0,5},{1,6},{2,7},{3,0},{4,1},{5,2},{6,3},{7,4},{8,13},{9,14},{10,... | collective-permute-start | bytes 786440 | tf_op jit(solution)/shard_map/ppermute | solution.py:530
  171.3 0.4 collective-permute-done.refs_0_
  171.6 2.2 collective-permute-start.5
  173.8 3.6 %collective-permute-start.6 = (bf16[256,512]{1,0:T(8,128)(2,1)}, bf16[256,512]{1,0:T(8,128)(2,1)}, u32[]{:S(2)}, u32[]{:S(2)}) collective-permute-start(bf16[256,512]{1,0:T(8,128)(2,1)} %get-tuple-element.65), channel_id=1, source_target_pairs={{0,7},{1,0},{2,1},{3,2},{4,3},{5,4},{6,5},{7,6},{8,15},{9,8},{10,9... | collective-permute-start | bytes 786440 | tf_op jit(solution)/shard_map/ppermute | solution.py:530
  177.4 23.7 %collective-permute-done.2.refs_2_ = bf16[256,512]{1,0:T(8,128)(2,1)S(1)} collective-permute-done((bf16[256,512]{1,0:T(8,128)(2,1)}, bf16[256,512]{1,0:T(8,128)(2,1)S(1)}, u32[]{:S(2)}, u32[]{:S(2)}) %collective-permute-start.2) | collective-permute-done | bytes 262176 | tf_op jit(solution)/shard_map/ppermute | solution.py:530
  201.1 0.6 copy-done.11
  201.7 0.6 fusion
  202.4 12.2 %prepare.1 = (bf16[256,2048]{1,0:T(8,128)(2,1)}, bf16[2048,256]{1,0:T(8,128)(2,1)}, bf16[2048,256]{1,0:T(8,128)(2,1)}, f32[2048,128]{1,0:T(8,128)}, f32[2048,128...) custom-call(s32[1]{0:T(128)} %bitcast.me_ref, bf16[8,272,512]{2,1,0:T(8,128)(2,1)} %all_to_all.15.refs_0_, ...), custom_call_target="tpu_custom_call" | custom-call | flops 536870912 | bytes 10485760 | tf_op jit(solution)/shard_map/prepare/pallas_call | solution.py:257
  214.6 2.5 collective-permute-start.16
  217.1 1.3 collective-permute-start.15
  218.4 8.2 %collective-permute-start.24 = (bf16[256,512]{1,0:T(8,128)(2,1)}, bf16[256,512]{1,0:T(8,128)(2,1)S(1)}, u32[]{:S(2)}, u32[]{:S(2)}) collective-permute-start(bf16[256,512]{1,0:T(8,128)(2,1)} %get-tuple-element.94), channel_id=1, source_target_pairs={{0,2},{1,3},{2,4},{3,5},{4,6},{5,7},{6,0},{7,1},{8,10},{9,11},{10,... | collective-permute-start | bytes 786440 | tf_op jit(solution)/shard_map/ppermute | solution.py:530
  226.7 4.2 %collective-permute-start.25 = (bf16[256,512]{1,0:T(8,128)(2,1)}, bf16[256,512]{1,0:T(8,128)(2,1)S(1)}, u32[]{:S(2)}, u32[]{:S(2)}) collective-permute-start(bf16[256,512]{1,0:T(8,128)(2,1)} %get-tuple-element.95), channel_id=1, source_target_pairs={{0,3},{1,4},{2,5},{3,6},{4,7},{5,0},{6,1},{7,2},{8,11},{9,12},{10,... | collective-permute-start | bytes 786440 | tf_op jit(solution)/shard_map/ppermute | solution.py:530
  230.9 3.2 collective-permute-start.27
  234.2 9.3 %convolve.4 = (bf16[2048,512]{1,0:T(8,128)(2,1)}, bf16[2048,512]{1,0:T(8,128)(2,1)}, bf16[2048,512]{1,0:T(8,128)(2,1)}, bf16[256,512]{1,0:T(8,128)(2,1)}) custom-call(s32[1]{0:T(128)} %bitcast.me_ref, bf16[256,16384]{1,0:T(8,128)(2,1)} %x_ref.11, bf16[256,512]{1,0:T(8,128)(2,1)} %copy-done.9, bf16[256,512]{1,0:T(8,128)(2,1)} %copy-done.10, ...), custom_call_target="tpu_custom_call" | custom-call | flops 536870912 | bytes 8388608 | tf_op jit(solution)/shard_map/convolve/pallas_call | solution.py:387
  243.5 2.0 collective-permute-start.19
  245.7 0.1 broadcast_in_dim_reshape.3
  245.8 2.0 collective-permute-start.18
  247.8 2.6 collective-permute-start.17
  250.4 9.2 %convolve.5 = (bf16[2048,512]{1,0:T(8,128)(2,1)}, bf16[2048,512]{1,0:T(8,128)(2,1)}, bf16[2048,512]{1,0:T(8,128)(2,1)}, bf16[256,512]{1,0:T(8,128)(2,1)}) custom-call(s32[1]{0:T(128)} %bitcast.me_ref, bf16[256,16384]{1,0:T(8,128)(2,1)} %x_ref.11, bf16[8,256,512]{2,1,0:T(8,128)(2,1)} %all-to-all-done.1.refs_0_, bf16[4,512]{1,0:T(4,128)(2,1)} %get-tuple-element.115.refs_1_, ...), custom_call_target="tpu_custom_call" | custom-call | flops 536870912 | bytes 8388608 | tf_op jit(solution)/shard_map/convolve/pallas_call | solution.py:387
  259.7 14.7 %collective-permute-start.28 = (bf16[256,512]{1,0:T(8,128)(2,1)}, bf16[256,512]{1,0:T(8,128)(2,1)}, u32[]{:S(2)}, u32[]{:S(2)}) collective-permute-start(bf16[256,512]{1,0:T(8,128)(2,1)} %get-tuple-element.98), channel_id=1, source_target_pairs={{0,6},{1,7},{2,0},{3,1},{4,2},{5,3},{6,4},{7,5},{8,14},{9,15},{10,... | collective-permute-start | bytes 786440 | tf_op jit(solution)/shard_map/ppermute | solution.py:530
  274.4 1.3 collective-permute-start.22
  275.7 0.6 fusion.1
  276.3 1.3 collective-permute-start.21
  277.7 1.3 collective-permute-start.20
  279.0 6.9 %emit.4 = (bf16[2048,2048]{1,0:T(8,128)(2,1)}, f32[8,128]{1,0:T(8,128)}) custom-call(bf16[2048,512]{1,0:T(8,128)(2,1)} %get-tuple-element.78.refs_0_, bf16[2048,512]{1,0:T(8,128)(2,1)} %get-tuple-element.79.refs_1_, bf16[2048,512]{1,0:T(8,128)(2,1)} %get-tuple-element.80.refs_2_, bf16[2048,256]{1,0:T(8,128)(2,1)} %get-tuple-element.81.refs_3_.refs_4_, ...), custom_call_target="tpu_custom_call" | custom-call | flops 1610612736 | bytes 11534336 | tf_op jit(solution)/shard_map/emit/pallas_call | solution.py:473
  285.9 9.3 %convolve.6 = (bf16[2048,512]{1,0:T(8,128)(2,1)}, bf16[2048,512]{1,0:T(8,128)(2,1)}, bf16[2048,512]{1,0:T(8,128)(2,1)}, bf16[256,512]{1,0:T(8,128)(2,1)}) custom-call(s32[1]{0:T(128)} %bitcast.me_ref, bf16[256,16384]{1,0:T(8,128)(2,1)} %x_ref.11, bf16[256,512]{1,0:T(8,128)(2,1)} %copy-done.6, bf16[256,512]{1,0:T(8,128)(2,1)} %copy-done.7, ...), custom_call_target="tpu_custom_call" | custom-call | flops 536870912 | bytes 8388608 | tf_op jit(solution)/shard_map/convolve/pallas_call | solution.py:387
  295.2 2.0 collective-permute-start.32
  297.2 2.0 collective-permute-start.31
  299.3 2.0 collective-permute-start.30
  301.3 0.7 copy-done.1
  302.0 0.1 copy-done.2
  302.1 6.9 %emit.5 = (bf16[2048,2048]{1,0:T(8,128)(2,1)}, f32[8,128]{1,0:T(8,128)}) custom-call(bf16[2048,2048]{1,0:T(8,128)(2,1)} %get-tuple-element.86.refs_0_, bf16[2048,512]{1,0:T(8,128)(2,1)} %get-tuple-element.88.refs_1_, bf16[2048,512]{1,0:T(8,128)(2,1)} %get-tuple-element.89.refs_2_, ...), custom_call_target="tpu_custom_call", output_to_operand_aliasing={{0}: (0, {})} | custom-call | flops 1610612736 | bytes 11534336 | tf_op jit(solution)/shard_map/emit/pallas_call | solution.py:473
  309.0 6.9 %emit.6 = (bf16[2048,2048]{1,0:T(8,128)(2,1)}, f32[8,128]{1,0:T(8,128)}) custom-call(bf16[2048,2048]{1,0:T(8,128)(2,1)} %get-tuple-element.92.refs_0_, bf16[2048,512]{1,0:T(8,128)(2,1)} %get-tuple-element.101.refs_1_, bf16[2048,512]{1,0:T(8,128)(2,1)} %get-tuple-element.102.refs_2_, ...), custom_call_target="tpu_custom_call", output_to_operand_aliasing={{0}: (0, {})} | custom-call | flops 1610612736 | bytes 11534336 | tf_op jit(solution)/shard_map/emit/pallas_call | solution.py:473
  315.9 9.3 %convolve.7 = (bf16[2048,512]{1,0:T(8,128)(2,1)}, bf16[2048,512]{1,0:T(8,128)(2,1)}, bf16[2048,512]{1,0:T(8,128)(2,1)}, bf16[256,512]{1,0:T(8,128)(2,1)}) custom-call(s32[1]{0:T(128)} %bitcast.me_ref, bf16[256,16384]{1,0:T(8,128)(2,1)} %x_ref.11, bf16[8,256,512]{2,1,0:T(8,128)(2,1)} %all-to-all-done.2.refs_0_, bf16[4,512]{1,0:T(4,128)(2,1)} %get-tuple-element.113.refs_1_, ...), custom_call_target="tpu_custom_call" | custom-call | flops 536870912 | bytes 8388608 | tf_op jit(solution)/shard_map/convolve/pallas_call | solution.py:387
  325.2 1.3 collective-permute-start.35
  326.6 3.9 %collective-permute-start.34 = (bf16[256,512]{1,0:T(8,128)(2,1)}, bf16[256,512]{1,0:T(8,128)(2,1)S(1)}, u32[]{:S(2)}, u32[]{:S(2)}) collective-permute-start(bf16[256,512]{1,0:T(8,128)(2,1)} %get-tuple-element.111), channel_id=1, source_target_pairs={{0,16},{8,24},{1,17},{9,25},{2,18},{10,26},{3,19},{11,27},{4,20},{... | collective-permute-start | bytes 786440 | tf_op jit(solution)/shard_map/ppermute | solution.py:535
  330.5 1.3 collective-permute-start.33
  331.8 1.6 collective-permute-done.35.refs_11_
  333.3 5.6 %collective-permute-done.34.refs_10_ = bf16[256,512]{1,0:T(8,128)(2,1)S(1)} collective-permute-done((bf16[256,512]{1,0:T(8,128)(2,1)}, bf16[256,512]{1,0:T(8,128)(2,1)S(1)}, u32[]{:S(2)}, u32[]{:S(2)}) %collective-permute-start.34) | collective-permute-done | bytes 262176 | tf_op jit(solution)/shard_map/ppermute | solution.py:535
  339.0 0.7 copy-done.4
  339.7 0.1 copy-done.5
  339.7 6.9 %emit.7 = (bf16[2048,2048]{1,0:T(8,128)(2,1)}, f32[8,128]{1,0:T(8,128)}) custom-call(bf16[2048,2048]{1,0:T(8,128)(2,1)} %get-tuple-element.105.refs_0_, bf16[2048,512]{1,0:T(8,128)(2,1)} %get-tuple-element.108.refs_1_, bf16[2048,512]{1,0:T(8,128)(2,1)} %get-tuple-element.109.refs_2_, ...), custom_call_target="tpu_custom_call", output_to_operand_aliasing={{0}: (0, {})} | custom-call | flops 1610612736 | bytes 11534336 | tf_op jit(solution)/shard_map/emit/pallas_call | solution.py:473
  (72 shorter events, 0.5 us)
Async XLA Ops:
  6.8 55.6 %all-to-all-start.1 = ((bf16[8,256,512]{2,1,0:T(8,128)(2,1)}), bf16[8,256,512]{2,1,0:T(8,128)(2,1)}, u32[]{:S(2)}, u32[]{:S(2)}) async-start(bf16[8,256,512]{2,1,0:T(8,128)(2,1)} %get-tuple-element.87), calls=%async_computation.1 | async-start | bytes 4194304 | tf_op jit(solution)/shard_map/all_to_all | solution.py:541
  117.8 198.1 %all-to-all-start.2 = ((bf16[8,256,512]{2,1,0:T(8,128)(2,1)}), bf16[8,256,512]{2,1,0:T(8,128)(2,1)}, u32[]{:S(2)}, u32[]{:S(2)}) async-start(bf16[8,256,512]{2,1,0:T(8,128)(2,1)} %get-tuple-element.106), calls=%async_computation.2 | async-start | bytes 4194304 | tf_op jit(solution)/shard_map/all_to_all | solution.py:541
  122.2 7.1 %copy-start.16 = (f32[256]{0:T(256)S(1)}, f32[256]{0:T(256)}, u32[]{:S(2)}) copy-start(f32[256]{0:T(256)} %param.14) | copy-start | bytes 3076
  122.2 7.1 %copy-start.17 = (f32[256]{0:T(256)S(1)}, f32[256]{0:T(256)}, u32[]{:S(2)}) copy-start(f32[256]{0:T(256)} %param.13) | copy-start | bytes 3076
  123.9 3.3 collective-permute-start.7
  124.6 3.4 collective-permute-start.8
  125.3 3.4 collective-permute-start.9
  125.9 4.9 %collective-permute-start.10 = (bf16[4,2560]{1,0:T(4,128)(2,1)}, bf16[4,2560]{1,0:T(4,128)(2,1)S(1)}, u32[]{:S(2)}, u32[]{:S(2)}) collective-permute-start(bf16[4,2560]{1,0:T(4,128)(2,1)} %get-tuple-element.69), channel_id=1, source_target_pairs={{7,11},{15,19},{23,27}} | collective-permute-start | bytes 61448 | tf_op jit(solution)/shard_map/ppermute | solution.py:556
  126.6 6.1 %collective-permute-start.11 = (bf16[4,2560]{1,0:T(4,128)(2,1)}, bf16[4,2560]{1,0:T(4,128)(2,1)S(1)}, u32[]{:S(2)}, u32[]{:S(2)}) collective-permute-start(bf16[4,2560]{1,0:T(4,128)(2,1)} %get-tuple-element.70), channel_id=1, source_target_pairs={{7,12},{15,20},{23,28}} | collective-permute-start | bytes 61448 | tf_op jit(solution)/shard_map/ppermute | solution.py:556
  127.3 6.9 %collective-permute-start.12 = (bf16[4,2560]{1,0:T(4,128)(2,1)}, bf16[4,2560]{1,0:T(4,128)(2,1)S(1)}, u32[]{:S(2)}, u32[]{:S(2)}) collective-permute-start(bf16[4,2560]{1,0:T(4,128)(2,1)} %get-tuple-element.71), channel_id=1, source_target_pairs={{7,13},{15,21},{23,29}} | collective-permute-start | bytes 61448 | tf_op jit(solution)/shard_map/ppermute | solution.py:556
  128.0 8.6 %collective-permute-start.13 = (bf16[4,2560]{1,0:T(4,128)(2,1)}, bf16[4,2560]{1,0:T(4,128)(2,1)S(1)}, u32[]{:S(2)}, u32[]{:S(2)}) collective-permute-start(bf16[4,2560]{1,0:T(4,128)(2,1)} %get-tuple-element.72), channel_id=1, source_target_pairs={{7,14},{15,22},{23,30}} | collective-permute-start | bytes 61448 | tf_op jit(solution)/shard_map/ppermute | solution.py:556
  128.7 38.8 %collective-permute-start.14 = (bf16[4,2560]{1,0:T(4,128)(2,1)}, bf16[4,2560]{1,0:T(4,128)(2,1)S(1)}, u32[]{:S(2)}, u32[]{:S(2)}) collective-permute-start(bf16[4,2560]{1,0:T(4,128)(2,1)} %get-tuple-element.73), channel_id=1, source_target_pairs={{7,15},{15,23},{23,31}} | collective-permute-start | bytes 61448 | tf_op jit(solution)/shard_map/ppermute | solution.py:556
  130.8 40.8 %collective-permute-start = (bf16[256,512]{1,0:T(8,128)(2,1)}, bf16[256,512]{1,0:T(8,128)(2,1)S(1)}, u32[]{:S(2)}, u32[]{:S(2)}) collective-permute-start(bf16[256,512]{1,0:T(8,128)(2,1)} %get-tuple-element.59), channel_id=1, source_target_pairs={{0,1},{1,2},{2,3},{3,4},{4,5},{5,6},{6,7},{7,0},{8,9},{9,10},{10,1... | collective-permute-start | bytes 786440 | tf_op jit(solution)/shard_map/ppermute | solution.py:530
  132.7 41.1 %collective-permute-start.1 = (bf16[256,512]{1,0:T(8,128)(2,1)}, bf16[256,512]{1,0:T(8,128)(2,1)S(1)}, u32[]{:S(2)}, u32[]{:S(2)}) collective-permute-start(bf16[256,512]{1,0:T(8,128)(2,1)} %get-tuple-element.60), channel_id=1, source_target_pairs={{0,2},{1,3},{2,4},{3,5},{4,6},{5,7},{6,0},{7,1},{8,10},{9,11},{10,... | collective-permute-start | bytes 786440 | tf_op jit(solution)/shard_map/ppermute | solution.py:530
  134.2 66.9 %collective-permute-start.2 = (bf16[256,512]{1,0:T(8,128)(2,1)}, bf16[256,512]{1,0:T(8,128)(2,1)S(1)}, u32[]{:S(2)}, u32[]{:S(2)}) collective-permute-start(bf16[256,512]{1,0:T(8,128)(2,1)} %get-tuple-element.61), channel_id=1, source_target_pairs={{0,3},{1,4},{2,5},{3,6},{4,7},{5,0},{6,1},{7,2},{8,11},{9,12},{10,... | collective-permute-start | bytes 786440 | tf_op jit(solution)/shard_map/ppermute | solution.py:530
  136.6 78.0 %collective-permute-start.3 = (bf16[256,512]{1,0:T(8,128)(2,1)}, bf16[256,512]{1,0:T(8,128)(2,1)S(1)}, u32[]{:S(2)}, u32[]{:S(2)}) collective-permute-start(bf16[256,512]{1,0:T(8,128)(2,1)} %get-tuple-element.62), channel_id=1, source_target_pairs={{0,4},{1,5},{2,6},{3,7},{4,0},{5,1},{6,2},{7,3},{8,12},{9,13},{10,... | collective-permute-start | bytes 786440 | tf_op jit(solution)/shard_map/ppermute | solution.py:530
  167.5 49.6 %collective-permute-start.4 = (bf16[256,512]{1,0:T(8,128)(2,1)}, bf16[256,512]{1,0:T(8,128)(2,1)S(1)}, u32[]{:S(2)}, u32[]{:S(2)}) collective-permute-start(bf16[256,512]{1,0:T(8,128)(2,1)} %get-tuple-element.63), channel_id=1, source_target_pairs={{0,5},{1,6},{2,7},{3,0},{4,1},{5,2},{6,3},{7,4},{8,13},{9,14},{10,... | collective-permute-start | bytes 786440 | tf_op jit(solution)/shard_map/ppermute | solution.py:530
  171.6 29.4 %copy-start.9 = (bf16[256,512]{1,0:T(8,128)(2,1)}, bf16[256,512]{1,0:T(8,128)(2,1)S(1)}, u32[]{:S(2)}) copy-start(bf16[256,512]{1,0:T(8,128)(2,1)S(1)} %collective-permute-done.refs_0_) | copy-start | bytes 786436
  171.6 46.8 %collective-permute-start.5 = (bf16[256,512]{1,0:T(8,128)(2,1)}, bf16[256,512]{1,0:T(8,128)(2,1)}, u32[]{:S(2)}, u32[]{:S(2)}) collective-permute-start(bf16[256,512]{1,0:T(8,128)(2,1)} %get-tuple-element.64), channel_id=1, source_target_pairs={{0,6},{1,7},{2,0},{3,1},{4,2},{5,3},{6,4},{7,5},{8,14},{9,15},{10,... | collective-permute-start | bytes 786440 | tf_op jit(solution)/shard_map/ppermute | solution.py:530
  173.8 27.2 %copy-start.10 = (bf16[256,512]{1,0:T(8,128)(2,1)}, bf16[256,512]{1,0:T(8,128)(2,1)S(1)}, u32[]{:S(2)}) copy-start(bf16[256,512]{1,0:T(8,128)(2,1)S(1)} %collective-permute-done.1.refs_1_) | copy-start | bytes 786436
  173.8 52.9 %collective-permute-start.6 = (bf16[256,512]{1,0:T(8,128)(2,1)}, bf16[256,512]{1,0:T(8,128)(2,1)}, u32[]{:S(2)}, u32[]{:S(2)}) collective-permute-start(bf16[256,512]{1,0:T(8,128)(2,1)} %get-tuple-element.65), channel_id=1, source_target_pairs={{0,7},{1,0},{2,1},{3,2},{4,3},{5,4},{6,5},{7,6},{8,15},{9,8},{10,9... | collective-permute-start | bytes 786440 | tf_op jit(solution)/shard_map/ppermute | solution.py:530
  201.0 0.7 copy-start.11
  201.1 42.4 %collective-permute-start.23 = (bf16[256,512]{1,0:T(8,128)(2,1)}, bf16[256,512]{1,0:T(8,128)(2,1)S(1)}, u32[]{:S(2)}, u32[]{:S(2)}) collective-permute-start(bf16[256,512]{1,0:T(8,128)(2,1)} %get-tuple-element.93), channel_id=1, source_target_pairs={{0,1},{1,2},{2,3},{3,4},{4,5},{5,6},{6,7},{7,0},{8,9},{9,10},{10,1... | collective-permute-start | bytes 786440 | tf_op jit(solution)/shard_map/ppermute | solution.py:530
  214.6 3.8 %copy-start.12 = (bf16[256,512]{1,0:T(8,128)(2,1)}, bf16[256,512]{1,0:T(8,128)(2,1)S(1)}, u32[]{:S(2)}) copy-start(bf16[256,512]{1,0:T(8,128)(2,1)S(1)} %collective-permute-done.3.refs_3_) | copy-start | bytes 786436
  214.6 16.3 %collective-permute-start.16 = (f32[8,128]{1,0:T(8,128)}, f32[8,128]{1,0:T(8,128)S(1)}, u32[]{:S(2)}, u32[]{:S(2)}) collective-permute-start(f32[8,128]{1,0:T(8,128)} %get-tuple-element.77), channel_id=1, source_target_pairs={{0,16},{8,24},{1,17},{9,25},{2,18},{10,26},{3,19},{11,27},{4,20},{... | collective-permute-start | bytes 12296 | tf_op jit(solution)/shard_map/ppermute | solution.py:535
  217.1 9.6 %copy-start.13 = (bf16[256,512]{1,0:T(8,128)(2,1)}, bf16[256,512]{1,0:T(8,128)(2,1)S(1)}, u32[]{:S(2)}) copy-start(bf16[256,512]{1,0:T(8,128)(2,1)S(1)} %collective-permute-done.4.refs_4_) | copy-start | bytes 786436
  217.1 13.8 %collective-permute-start.15 = (f32[8,128]{1,0:T(8,128)}, f32[8,128]{1,0:T(8,128)S(1)}, u32[]{:S(2)}, u32[]{:S(2)}) collective-permute-start(f32[8,128]{1,0:T(8,128)} %get-tuple-element.77), channel_id=1, source_target_pairs={{0,8},{8,16},{16,24},{1,9},{9,17},{17,25},{2,10},{10,18},{18,26},{... | collective-permute-start | bytes 12296 | tf_op jit(solution)/shard_map/ppermute | solution.py:535
  218.4 27.3 %collective-permute-start.24 = (bf16[256,512]{1,0:T(8,128)(2,1)}, bf16[256,512]{1,0:T(8,128)(2,1)S(1)}, u32[]{:S(2)}, u32[]{:S(2)}) collective-permute-start(bf16[256,512]{1,0:T(8,128)(2,1)} %get-tuple-element.94), channel_id=1, source_target_pairs={{0,2},{1,3},{2,4},{3,5},{4,6},{5,7},{6,0},{7,1},{8,10},{9,11},{10,... | collective-permute-start | bytes 786440 | tf_op jit(solution)/shard_map/ppermute | solution.py:530
  226.7 21.1 %collective-permute-start.25 = (bf16[256,512]{1,0:T(8,128)(2,1)}, bf16[256,512]{1,0:T(8,128)(2,1)S(1)}, u32[]{:S(2)}, u32[]{:S(2)}) collective-permute-start(bf16[256,512]{1,0:T(8,128)(2,1)} %get-tuple-element.95), channel_id=1, source_target_pairs={{0,3},{1,4},{2,5},{3,6},{4,7},{5,0},{6,1},{7,2},{8,11},{9,12},{10,... | collective-permute-start | bytes 786440 | tf_op jit(solution)/shard_map/ppermute | solution.py:530
  230.9 3.3 copy-start.14
  230.9 28.8 %collective-permute-start.26 = (bf16[256,512]{1,0:T(8,128)(2,1)}, bf16[256,512]{1,0:T(8,128)(2,1)}, u32[]{:S(2)}, u32[]{:S(2)}) collective-permute-start(bf16[256,512]{1,0:T(8,128)(2,1)} %get-tuple-element.96), channel_id=1, source_target_pairs={{0,4},{1,5},{2,6},{3,7},{4,0},{5,1},{6,2},{7,3},{8,12},{9,13},{10,... | collective-permute-start | bytes 786440 | tf_op jit(solution)/shard_map/ppermute | solution.py:530
  230.9 3.2 copy-start.15
  230.9 43.5 %collective-permute-start.27 = (bf16[256,512]{1,0:T(8,128)(2,1)}, bf16[256,512]{1,0:T(8,128)(2,1)}, u32[]{:S(2)}, u32[]{:S(2)}) collective-permute-start(bf16[256,512]{1,0:T(8,128)(2,1)} %get-tuple-element.97), channel_id=1, source_target_pairs={{0,5},{1,6},{2,7},{3,0},{4,1},{5,2},{6,3},{7,4},{8,13},{9,14},{10,... | collective-permute-start | bytes 786440 | tf_op jit(solution)/shard_map/ppermute | solution.py:530
  234.2 11.3 %copy-start.18 = (f32[256]{0:T(256)S(1)}, f32[256]{0:T(256)}, u32[]{:S(2)}) copy-start(f32[256]{0:T(256)} %param.15) | copy-start | bytes 3076
  243.5 16.1 %copy-start.6 = (bf16[256,512]{1,0:T(8,128)(2,1)}, bf16[256,512]{1,0:T(8,128)(2,1)S(1)}, u32[]{:S(2)}) copy-start(bf16[256,512]{1,0:T(8,128)(2,1)S(1)} %collective-permute-done.23.refs_0_) | copy-start | bytes 786436
  243.5 30.9 %collective-permute-start.19 = (bf16[256,512]{1,0:T(8,128)(2,1)}, bf16[256,512]{1,0:T(8,128)(2,1)}, u32[]{:S(2)}, u32[]{:S(2)}) collective-permute-start(bf16[256,512]{1,0:T(8,128)(2,1)} %get-tuple-element.85), channel_id=1, source_target_pairs={{0,24},{1,25},{2,26},{3,27},{4,28},{5,29},{6,30},{7,31}} | collective-permute-start | bytes 786440 | tf_op jit(solution)/shard_map/ppermute | solution.py:535
  245.7 13.9 %copy-start.7 = (bf16[256,512]{1,0:T(8,128)(2,1)}, bf16[256,512]{1,0:T(8,128)(2,1)S(1)}, u32[]{:S(2)}) copy-start(bf16[256,512]{1,0:T(8,128)(2,1)S(1)} %collective-permute-done.24.refs_1_) | copy-start | bytes 786436
  245.8 30.6 %collective-permute-start.18 = (bf16[256,512]{1,0:T(8,128)(2,1)}, bf16[256,512]{1,0:T(8,128)(2,1)}, u32[]{:S(2)}, u32[]{:S(2)}) collective-permute-start(bf16[256,512]{1,0:T(8,128)(2,1)} %get-tuple-element.85), channel_id=1, source_target_pairs={{0,16},{8,24},{1,17},{9,25},{2,18},{10,26},{3,19},{11,27},{4,20},{... | collective-permute-start | bytes 786440 | tf_op jit(solution)/shard_map/ppermute | solution.py:535
  247.8 11.9 %copy-start.8 = (bf16[256,512]{1,0:T(8,128)(2,1)}, bf16[256,512]{1,0:T(8,128)(2,1)S(1)}, u32[]{:S(2)}) copy-start(bf16[256,512]{1,0:T(8,128)(2,1)S(1)} %collective-permute-done.25.refs_2_) | copy-start | bytes 786436
  247.8 29.8 %collective-permute-start.17 = (bf16[256,512]{1,0:T(8,128)(2,1)}, bf16[256,512]{1,0:T(8,128)(2,1)}, u32[]{:S(2)}, u32[]{:S(2)}) collective-permute-start(bf16[256,512]{1,0:T(8,128)(2,1)} %get-tuple-element.85), channel_id=1, source_target_pairs={{0,8},{8,16},{16,24},{1,9},{9,17},{17,25},{2,10},{10,18},{18,26},{... | collective-permute-start | bytes 786440 | tf_op jit(solution)/shard_map/ppermute | solution.py:535
  259.7 26.2 %collective-permute-start.28 = (bf16[256,512]{1,0:T(8,128)(2,1)}, bf16[256,512]{1,0:T(8,128)(2,1)}, u32[]{:S(2)}, u32[]{:S(2)}) collective-permute-start(bf16[256,512]{1,0:T(8,128)(2,1)} %get-tuple-element.98), channel_id=1, source_target_pairs={{0,6},{1,7},{2,0},{3,1},{4,2},{5,3},{6,4},{7,5},{8,14},{9,15},{10,... | collective-permute-start | bytes 786440 | tf_op jit(solution)/shard_map/ppermute | solution.py:530
  274.4 11.5 %collective-permute-start.29 = (bf16[256,512]{1,0:T(8,128)(2,1)}, bf16[256,512]{1,0:T(8,128)(2,1)}, u32[]{:S(2)}, u32[]{:S(2)}) collective-permute-start(bf16[256,512]{1,0:T(8,128)(2,1)} %get-tuple-element.99), channel_id=1, source_target_pairs={{0,7},{1,0},{2,1},{3,2},{4,3},{5,4},{6,5},{7,6},{8,15},{9,8},{10,9... | collective-permute-start | bytes 786440 | tf_op jit(solution)/shard_map/ppermute | solution.py:530
  274.4 24.8 %collective-permute-start.22 = (bf16[256,512]{1,0:T(8,128)(2,1)}, bf16[256,512]{1,0:T(8,128)(2,1)S(1)}, u32[]{:S(2)}, u32[]{:S(2)}) collective-permute-start(bf16[256,512]{1,0:T(8,128)(2,1)} %get-tuple-element.91), channel_id=1, source_target_pairs={{0,24},{1,25},{2,26},{3,27},{4,28},{5,29},{6,30},{7,31}} | collective-permute-start | bytes 786440 | tf_op jit(solution)/shard_map/ppermute | solution.py:535
  276.3 24.9 %collective-permute-start.21 = (bf16[256,512]{1,0:T(8,128)(2,1)}, bf16[256,512]{1,0:T(8,128)(2,1)S(1)}, u32[]{:S(2)}, u32[]{:S(2)}) collective-permute-start(bf16[256,512]{1,0:T(8,128)(2,1)} %get-tuple-element.91), channel_id=1, source_target_pairs={{0,16},{8,24},{1,17},{9,25},{2,18},{10,26},{3,19},{11,27},{4,20},{... | collective-permute-start | bytes 786440 | tf_op jit(solution)/shard_map/ppermute | solution.py:535
  277.7 23.6 %collective-permute-start.20 = (bf16[256,512]{1,0:T(8,128)(2,1)}, bf16[256,512]{1,0:T(8,128)(2,1)S(1)}, u32[]{:S(2)}, u32[]{:S(2)}) collective-permute-start(bf16[256,512]{1,0:T(8,128)(2,1)} %get-tuple-element.91), channel_id=1, source_target_pairs={{0,8},{8,16},{16,24},{1,9},{9,17},{17,25},{2,10},{10,18},{18,26},{... | collective-permute-start | bytes 786440 | tf_op jit(solution)/shard_map/ppermute | solution.py:535
  295.2 13.8 %collective-permute-start.32 = (bf16[256,512]{1,0:T(8,128)(2,1)}, bf16[256,512]{1,0:T(8,128)(2,1)}, u32[]{:S(2)}, u32[]{:S(2)}) collective-permute-start(bf16[256,512]{1,0:T(8,128)(2,1)} %get-tuple-element.104), channel_id=1, source_target_pairs={{0,24},{1,25},{2,26},{3,27},{4,28},{5,29},{6,30},{7,31}} | collective-permute-start | bytes 786440 | tf_op jit(solution)/shard_map/ppermute | solution.py:535
  297.2 11.7 %collective-permute-start.31 = (bf16[256,512]{1,0:T(8,128)(2,1)}, bf16[256,512]{1,0:T(8,128)(2,1)}, u32[]{:S(2)}, u32[]{:S(2)}) collective-permute-start(bf16[256,512]{1,0:T(8,128)(2,1)} %get-tuple-element.104), channel_id=1, source_target_pairs={{0,16},{8,24},{1,17},{9,25},{2,18},{10,26},{3,19},{11,27},{4,20},{... | collective-permute-start | bytes 786440 | tf_op jit(solution)/shard_map/ppermute | solution.py:535
  299.3 2.0 copy-start
  299.3 9.7 %collective-permute-start.30 = (bf16[256,512]{1,0:T(8,128)(2,1)}, bf16[256,512]{1,0:T(8,128)(2,1)}, u32[]{:S(2)}, u32[]{:S(2)}) collective-permute-start(bf16[256,512]{1,0:T(8,128)(2,1)} %get-tuple-element.104), channel_id=1, source_target_pairs={{0,8},{8,16},{16,24},{1,9},{9,17},{17,25},{2,10},{10,18},{18,26},{... | collective-permute-start | bytes 786440 | tf_op jit(solution)/shard_map/ppermute | solution.py:535
  301.3 0.7 copy-start.1
  301.3 0.8 copy-start.2
  325.2 8.1 %collective-permute-start.35 = (bf16[256,512]{1,0:T(8,128)(2,1)}, bf16[256,512]{1,0:T(8,128)(2,1)S(1)}, u32[]{:S(2)}, u32[]{:S(2)}) collective-permute-start(bf16[256,512]{1,0:T(8,128)(2,1)} %get-tuple-element.111), channel_id=1, source_target_pairs={{0,24},{1,25},{2,26},{3,27},{4,28},{5,29},{6,30},{7,31}} | collective-permute-start | bytes 786440 | tf_op jit(solution)/shard_map/ppermute | solution.py:535
  326.6 12.4 %collective-permute-start.34 = (bf16[256,512]{1,0:T(8,128)(2,1)}, bf16[256,512]{1,0:T(8,128)(2,1)S(1)}, u32[]{:S(2)}, u32[]{:S(2)}) collective-permute-start(bf16[256,512]{1,0:T(8,128)(2,1)} %get-tuple-element.111), channel_id=1, source_target_pairs={{0,16},{8,24},{1,17},{9,25},{2,18},{10,26},{3,19},{11,27},{4,20},{... | collective-permute-start | bytes 786440 | tf_op jit(solution)/shard_map/ppermute | solution.py:535
  330.5 8.5 %collective-permute-start.33 = (bf16[256,512]{1,0:T(8,128)(2,1)}, bf16[256,512]{1,0:T(8,128)(2,1)S(1)}, u32[]{:S(2)}, u32[]{:S(2)}) collective-permute-start(bf16[256,512]{1,0:T(8,128)(2,1)} %get-tuple-element.111), channel_id=1, source_target_pairs={{0,8},{8,16},{16,24},{1,9},{9,17},{17,25},{2,10},{10,18},{18,26},{... | collective-permute-start | bytes 786440 | tf_op jit(solution)/shard_map/ppermute | solution.py:535
  333.3 5.6 %copy-start.3 = (bf16[256,512]{1,0:T(8,128)(2,1)}, bf16[256,512]{1,0:T(8,128)(2,1)S(1)}, u32[]{:S(2)}) copy-start(bf16[256,512]{1,0:T(8,128)(2,1)S(1)} %collective-permute-done.35.refs_11_) | copy-start | bytes 786436
  338.9 0.7 copy-start.4
  338.9 0.8 copy-start.5

commit v2 on v1

--- a/solution.py
+++ b/solution.py
@@ -35,7 +35,11 @@
 
 
 def chunk_widths(channels):
-    return [channels // 4] * 4
+    return [channels // 8 * part for part in (2, 2, 2, 2)]
+
+
+def group_width(width):
+    return 256 if width % 256 == 0 else LANES
 
 
 def rows_ahead(edge_ref):
@@ -97,7 +101,7 @@
 
 
 def by_permutes(k):
-    return k % 2 == 0
+    return k != 2
 
 
 def pack_x(me, x_in, n, channels, widths):
@@ -287,7 +291,7 @@
     tok = x_in.shape[0]
     total = n * tok
     got_count = len(received)
-    group = min(width, 256)
+    group = group_width(width)
     strip = 64
     lead = 2 * EDGE_ROWS
 
@@ -316,7 +320,7 @@
         decs[...] = spread(dj_ref[: decs.shape[0], :], first // HEADDIM, width)
         e = rows_ahead(edge_ref)
         for g in range(width // LANES):
-            xf_buf[g, EDGE_ROWS:lead, :] = e[:, g * LANES : (g + 1) * LANES]
+            xf_buf[g, EDGE_ROWS:lead, :] = e[:, first + g * LANES : first + (g + 1) * LANES]
         state[...] = jnp.zeros_like(state)
 
         def outgoing(j):
@@ -343,13 +347,14 @@
                 per_head = wu_ref[pl.ds(r, strip), :]
                 for g in range(width // LANES):
                     cols = slice(g * LANES, (g + 1) * LANES)
+                    here = slice(first + g * LANES, first + (g + 1) * LANES)
                     low = lead + i * strip
                     x = x_buf[pl.ds(r, strip), cols].astype(F32)
                     xf_buf[g, low : low + strip, :] = x
-                    acc = b_ref[:, cols] + w_ref[CONV - 1 :, cols] * x
+                    acc = b_ref[:, here] + w_ref[CONV - 1 :, here] * x
                     for back in range(1, CONV):
                         acc = acc + (
-                            w_ref[CONV - 1 - back : CONV - back, cols]
+                            w_ref[CONV - 1 - back : CONV - back, here]
                             * xf_buf[g, low - back : low - back + strip, :]
                         )
                     xc = silu(acc).astype(BF16)
@@ -375,15 +380,6 @@
             for copy in outgoing(j):
                 copy.wait()
 
-    def columns(rows):
-        per = channels // width if channels % width == 0 and first % width == 0 else 0
-        if per:
-            return pl.BlockSpec((rows, width), lambda i, me: (0, me[0] * per + first // width))
-        return pl.BlockSpec(
-            (pl.Element(rows), pl.Element(width)),
-            lambda i, me: (0, pl.multiple_of(me[0] * channels + first, LANES)),
-        )
-
     return pl.pallas_call(
         body,
         grid_spec=pltpu.PrefetchScalarGridSpec(
@@ -391,9 +387,9 @@
             grid=(1,),
             in_specs=[ANY] * (1 + got_count)
             + [
-                whole((SENT_ROWS, width)),
-                columns(CONV),
-                columns(1),
+                whole(edge.shape),
+                whole(weight.shape),
+                whole(bias.shape),
                 whole(bt.shape),
                 whole(wu.shape),
                 whole(dj.shape),
@@ -427,10 +423,10 @@
 def emit(y, xc, u, s_loc, c, m, ec, pj, ends, decays, skip, channels, width, first):
     total = xc.shape[0]
     tok = m.shape[1]
-    group = min(width, 256)
+    group = group_width(width)
     n_ends, n_decays = len(ends), len(decays)
     alias = [] if y is None else [y]
-    fold = 2
+    fold = 4
 
     def body(*refs):
         refs = refs[len(alias) :]
@@ -459,7 +455,8 @@
                 acc += jnp.dot(c_ref[rows, :], s.astype(BF16), preferred_element_type=F32)
                 e = spread(ec_ref[rows, :], (first + g * group) // HEADDIM, group)
                 x = xc_ref[rows, cols].astype(F32)
-                out_ref[rows, cols] = (e * acc + skip_ref[:, cols] * x).astype(BF16)
+                here = slice(first + g * group, first + (g + 1) * group)
+                out_ref[rows, cols] = (e * acc + skip_ref[:, here] * x).astype(BF16)
 
     def ahead(shape):
         return pl.BlockSpec((fold * shape[0], shape[1]), lambda j: (j, 0))
@@ -482,7 +479,7 @@
             ahead((tok, tok)),
             ahead((tok, LANES)),
             whole(pj.shape),
-            whole((1, width)),
+            whole(skip.shape),
         ]
         + [whole((STATE, width))] * n_ends
         + [whole((EDGE_ROWS, LANES))] * n_decays,
@@ -549,8 +546,6 @@
     widths = chunk_widths(channels)
     packed = pack_bc(bc_in, dt_raw, n, heads_dev, per_group)
     message = exchange(packed)
-    packed_x = pack_x(me, x_in, n, channels, widths)
-    received = [send(k, parts) for k, parts in enumerate(packed_x)]
     edges = pack_edge(x_in, bc_in, n, channels, heads_dev, per_group)
     edges = [
         lax.ppermute(
@@ -558,8 +553,12 @@
         )
         for j, e in enumerate(edges)
     ]
+    packed_x = pack_x(me, x_in, n, channels, widths)
+    received = [send(k, parts) for k, parts in enumerate(packed_x)]
+    skip = jnp.repeat(mine(d_skip), HEADDIM)[None, :]
+    x_weight = lax.dynamic_slice_in_dim(conv_x_weight, index * channels, channels, 1)
+    x_bias = lax.dynamic_slice_in_dim(conv_x_bias, index * channels, channels, 0)[None, :]
     edge = sum(edges)
-    skip = jnp.repeat(mine(d_skip), HEADDIM)[None, :]
     bt, c, m, wu, ec, dj, pj, dv = prepare(
         me,
         message,
@@ -578,22 +577,8 @@
 
     def finish():
         k, xc, u, s_loc, ends = pending.pop(0)
-        cut = slice(sum(widths[:k]), sum(widths[: k + 1]))
         return emit(
-            y,
-            xc,
-            u,
-            s_loc,
-            c,
-            m,
-            ec,
-            pj,
-            ends,
-            decays,
-            skip[:, cut],
-            channels,
-            widths[k],
-            cut.start,
+            y, xc, u, s_loc, c, m, ec, pj, ends, decays, skip, channels, widths[k], sum(widths[:k])
         )
 
     last = len(widths) - 1
@@ -603,9 +588,9 @@
             me,
             x_in,
             received[k],
-            edge[:, first : first + width],
-            conv_x_weight,
-            conv_x_bias[None, :],
+            edge,
+            x_weight,
+            x_bias,
             bt,
             wu,
             dj,
@@ -617,7 +602,7 @@
         )
         ends = [forward(end, by) for by in range(1, n_slab)]
         pending.append((k, xc, u, s_loc, ends))
-        while pending and (len(pending) > 1 or k >= last - 1):
+        while pending and (len(pending) > 1 or k in (0, last)):
             y, token = finish()
             tokens.append(token)
     return y

time: 348 us -> 311 us (0.89)
  blocking collectives: 55.3 us -> 0 us
  waiting for transfers between devices: 76.5 us -> 97.4 us
  Pallas kernels: 88.7 us -> 84.9 us
    all_to_all x1 -> x0, blocking collectives: 55.3 us -> none  [exchange(): return lax.all_to_all(a, 'inner', split_axis=0, concat_axis=0, tiled=True)]
    ppermute x14 -> x21, waiting for transfers between devices: 24.1 us -> 53 us  [rotate(): lax.ppermute(arrays[s - 1], 'inner', [(i, (i + s) % n) for i in range(n)])]
    ppermute x14, waiting for transfers between devices: 7.2 us -> 0.04 us  [forward(): return lax.ppermute(a, 'slab', [(i, i + by) for i in range(n_slab - by)])]
    pallas_call x4, Pallas kernels: 27.7 us -> 23.9 us  [emit(): pl.pallas_call(body, grid=(total // (fold * tok),), in_specs=[ANY] * len(...]
    ppermute x14 -> x21, starting transfers between devices: 76.6 us -> 76.9 us  [rotate(): lax.ppermute(arrays[s - 1], 'inner', [(i, (i + s) % n) for i in range(n)])]
  transfers between devices with their start and end apart: 38 -> 45, of which waited for: 5 -> 5; matrix products, arithmetic and copies ran while one was open for 1% -> 2% of each run, Pallas kernels for 19% -> 25%
where the time goes in v2:
time: 311 us; the launch traced here: 308 us
  starting transfers between devices  119 us (38%)
  waiting for transfers between devices  97.4 us (31%)
  Pallas kernels  84.9 us (27%)
  local copies, waits for them, and re-layouts  6.21 us (2%)
    ppermute x21, starting transfers between devices, rotate(): lax.ppermute(arrays[s - 1], 'inner', [(i, (i + s) % n) for i in range(n)])  76.9 us
    ppermute x21, waiting for transfers between devices, rotate(): lax.ppermute(arrays[s - 1], 'inner', [(i, (i + s) % n) for i in range(n)])  53 us
    all_to_all x2, waiting for transfers between devices, exchange(): return lax.all_to_all(a, 'inner', split_axis=0, concat_axis=0, tiled=True)  44.4 us
    pallas_call x4, Pallas kernels, convolve(): pl.pallas_call(body, grid_spec=pltpu.PrefetchScalarGridSpec(num_scalar_pr...  37.1 us
    ppermute x14, starting transfers between devices, forward(): return lax.ppermute(a, 'slab', [(i, i + by) for i in range(n_slab - by)])  25.6 us
    pallas_call x4, Pallas kernels, emit(): pl.pallas_call(body, grid=(total // (fold * tok),), in_specs=[ANY] * len(...  23.9 us
    pallas_call x1, Pallas kernels, prepare(): pl.pallas_call(body, grid_spec=pltpu.PrefetchScalarGridSpec(num_scalar_pr...  12.2 us
    all_to_all x2, starting transfers between devices, exchange(): return lax.all_to_all(a, 'inner', split_axis=0, concat_axis=0, tiled=True)  11.6 us
  transfers between devices with their start and end apart: 45, of which 5 were waited for; matrix products, arithmetic and copies ran while one was open for 2% of the time, Pallas kernels for 25%

profile of v2, /device:TPU:0, one launch (start us, length us, event | category | flops | bytes accessed | tf_op | source)
XLA Modules:
  0.0 308.5 jit_solution(10186868079976326836)
XLA Ops:
  0.0 3.2 %pack_bc.1 = bf16[8,272,512]{2,1,0:T(8,128)(2,1)} custom-call(bf16[256,4096]{1,0:T(8,128)(2,1)} %bc_ref.3, bf16[256,256]{1,0:T(8,128)(2,1)} %dt_ref.1), custom_call_target="tpu_custom_call" | custom-call | bytes 4194304 | tf_op jit(solution)/shard_map/pack_bc/pallas_call | solution.py:91
  3.2 7.3 %all-to-all-start = ((bf16[8,272,512]{2,1,0:T(8,128)(2,1)}), bf16[8,272,512]{2,1,0:T(8,128)(2,1)}, u32[]{:S(2)}, u32[]{:S(2)}) async-start(bf16[8,272,512]{2,1,0:T(8,128)(2,1)} %pack_bc.1), calls=%async_computation | async-start | bytes 4456448 | tf_op jit(solution)/shard_map/all_to_all | solution.py:538
  10.5 6.8 %pack_x.1 = (bf16[256,512]{1,0:T(8,128)(2,1)}, bf16[256,512]{1,0:T(8,128)(2,1)}, bf16[256,512]{1,0:T(8,128)(2,1)}, bf16[256,512]{1,0:T(8,128)(2,1)}, bf16[256,51...) custom-call(s32[1]{0:T(128)} %bitcast.me_ref, ...), custom_call_target="tpu_custom_call" | custom-call | bytes 16777216 | tf_op jit(solution)/shard_map/pack_x/pallas_call | solution.py:133
  17.2 44.4 %all-to-all-done.refs_0_ = bf16[8,272,512]{2,1,0:T(8,128)(2,1)} async-done(((bf16[8,272,512]{2,1,0:T(8,128)(2,1)}), bf16[8,272,512]{2,1,0:T(8,128)(2,1)}, u32[]{:S(2)}, u32[]{:S(2)}) %all-to-all-start) | async-done | bytes 2228256 | tf_op jit(solution)/shard_map/all_to_all | solution.py:538
  61.6 4.4 %all-to-all-start.1 = ((bf16[8,256,512]{2,1,0:T(8,128)(2,1)}), bf16[8,256,512]{2,1,0:T(8,128)(2,1)}, u32[]{:S(2)}, u32[]{:S(2)}) async-start(bf16[8,256,512]{2,1,0:T(8,128)(2,1)} %get-tuple-element.106), calls=%async_computation.1 | async-start | bytes 4194304 | tf_op jit(solution)/shard_map/all_to_all | solution.py:538
  66.0 1.9 collective-permute-start
  67.9 1.5 collective-permute-start.1
  69.4 2.4 collective-permute-start.2
  71.7 1.7 pack_edge.1
  73.5 0.7 collective-permute-start.14
  74.1 0.7 collective-permute-start.13
  74.8 0.7 collective-permute-start.12
  75.5 0.7 collective-permute-start.11
  76.2 0.7 collective-permute-start.10
  76.8 0.7 collective-permute-start.9
  77.5 0.7 collective-permute-start.7
  78.2 0.7 collective-permute-start.8
  79.0 0.7 copy.14.refs_6_
  79.7 0.7 copy.15.refs_7_
  80.4 1.4 collective-permute-start.3
  81.8 2.4 collective-permute-start.4
  84.2 27.6 %collective-permute-done.refs_0_ = bf16[256,512]{1,0:T(8,128)(2,1)S(1)} collective-permute-done((bf16[256,512]{1,0:T(8,128)(2,1)}, bf16[256,512]{1,0:T(8,128)(2,1)S(1)}, u32[]{:S(2)}, u32[]{:S(2)}) %collective-permute-start) | collective-permute-done | bytes 262176 | tf_op jit(solution)/shard_map/ppermute | solution.py:527
  111.8 19.6 %collective-permute-start.5 = (bf16[256,512]{1,0:T(8,128)(2,1)}, bf16[256,512]{1,0:T(8,128)(2,1)}, u32[]{:S(2)}, u32[]{:S(2)}) collective-permute-start(bf16[256,512]{1,0:T(8,128)(2,1)} %get-tuple-element.70), channel_id=1, source_target_pairs={{0,6},{1,7},{2,0},{3,1},{4,2},{5,3},{6,4},{7,5},{8,14},{9,15},{10,... | collective-permute-start | bytes 786440 | tf_op jit(solution)/shard_map/ppermute | solution.py:527
  131.4 14.3 %collective-permute-done.2.refs_2_ = bf16[256,512]{1,0:T(8,128)(2,1)} collective-permute-done((bf16[256,512]{1,0:T(8,128)(2,1)}, bf16[256,512]{1,0:T(8,128)(2,1)}, u32[]{:S(2)}, u32[]{:S(2)}) %collective-permute-start.2) | collective-permute-done | bytes 262176 | tf_op jit(solution)/shard_map/ppermute | solution.py:527
  146.3 12.2 %prepare.1 = (bf16[256,2048]{1,0:T(8,128)(2,1)}, bf16[2048,256]{1,0:T(8,128)(2,1)}, bf16[2048,256]{1,0:T(8,128)(2,1)}, f32[2048,128]{1,0:T(8,128)}, f32[2048,128...) custom-call(s32[1]{0:T(128)} %bitcast.me_ref, ...), custom_call_target="tpu_custom_call" | custom-call | flops 536870912 | bytes 10485760 | tf_op jit(solution)/shard_map/prepare/pallas_call | solution.py:261
  158.6 1.3 collective-permute-start.15
  159.9 3.2 %collective-permute-start.16 = (f32[8,128]{1,0:T(8,128)}, f32[8,128]{1,0:T(8,128)S(1)}, u32[]{:S(2)}, u32[]{:S(2)}) collective-permute-start(f32[8,128]{1,0:T(8,128)} %get-tuple-element.83), channel_id=1, source_target_pairs={{0,16},{8,24},{1,17},{9,25},{2,18},{10,26},{3,19},{11,27},{4,20},{... | collective-permute-start | bytes 12296 | tf_op jit(solution)/shard_map/ppermute | solution.py:532
  163.1 8.7 %collective-permute-start.21 = (bf16[256,512]{1,0:T(8,128)(2,1)}, bf16[256,512]{1,0:T(8,128)(2,1)}, u32[]{:S(2)}, u32[]{:S(2)}) collective-permute-start(bf16[256,512]{1,0:T(8,128)(2,1)} %get-tuple-element.94), channel_id=1, source_target_pairs={{0,2},{1,3},{2,4},{3,5},{4,6},{5,7},{6,0},{7,1},{8,10},{9,11},{10,... | collective-permute-start | bytes 786440 | tf_op jit(solution)/shard_map/ppermute | solution.py:527
  171.8 4.3 %collective-permute-start.22 = (bf16[256,512]{1,0:T(8,128)(2,1)}, bf16[256,512]{1,0:T(8,128)(2,1)}, u32[]{:S(2)}, u32[]{:S(2)}) collective-permute-start(bf16[256,512]{1,0:T(8,128)(2,1)} %get-tuple-element.95), channel_id=1, source_target_pairs={{0,3},{1,4},{2,5},{3,6},{4,7},{5,0},{6,1},{7,2},{8,11},{9,12},{10,... | collective-permute-start | bytes 786440 | tf_op jit(solution)/shard_map/ppermute | solution.py:527
  176.1 2.3 collective-permute-start.24
  179.2 1.3 dynamic_slice.16
  180.6 9.3 %convolve.4 = (bf16[2048,512]{1,0:T(8,128)(2,1)}, bf16[2048,512]{1,0:T(8,128)(2,1)}, bf16[2048,512]{1,0:T(8,128)(2,1)}, bf16[256,512]{1,0:T(8,128)(2,1)}) custom-call(s32[1]{0:T(128)} %bitcast.me_ref, bf16[256,16384]{1,0:T(8,128)(2,1)} %x_ref.11, bf16[256,512]{1,0:T(8,128)(2,1)} %copy-done.7, bf16[256,512]{1,0:T(8,128)(2,1)} %copy-done.8, ...), custom_call_target="tpu_custom_call" | custom-call | flops 536870912 | bytes 8388608 | tf_op jit(solution)/shard_map/convolve/pallas_call | solution.py:383
  189.9 3.4 %collective-permute-start.26 = (bf16[256,512]{1,0:T(8,128)(2,1)}, bf16[256,512]{1,0:T(8,128)(2,1)S(1)}, u32[]{:S(2)}, u32[]{:S(2)}) collective-permute-start(bf16[256,512]{1,0:T(8,128)(2,1)} %get-tuple-element.99), channel_id=1, source_target_pairs={{0,7},{1,0},{2,1},{3,2},{4,3},{5,4},{6,5},{7,6},{8,15},{9,8},{10,9... | collective-permute-start | bytes 786440 | tf_op jit(solution)/shard_map/ppermute | solution.py:527
  193.3 2.0 collective-permute-start.17
  195.3 7.8 %collective-permute-done.23.refs_3_ = bf16[256,512]{1,0:T(8,128)(2,1)} collective-permute-done((bf16[256,512]{1,0:T(8,128)(2,1)}, bf16[256,512]{1,0:T(8,128)(2,1)}, u32[]{:S(2)}, u32[]{:S(2)}) %collective-permute-start.23) | collective-permute-done | bytes 262176 | tf_op jit(solution)/shard_map/ppermute | solution.py:527
  203.0 2.0 collective-permute-start.18
  205.0 2.0 collective-permute-start.19
  207.0 5.0 %collective-permute-start.33 = (bf16[256,512]{1,0:T(8,128)(2,1)}, bf16[256,512]{1,0:T(8,128)(2,1)S(1)}, u32[]{:S(2)}, u32[]{:S(2)}) collective-permute-start(bf16[256,512]{1,0:T(8,128)(2,1)} %get-tuple-element.112), channel_id=1, source_target_pairs={{0,1},{1,2},{2,3},{3,4},{4,5},{5,6},{6,7},{7,0},{8,9},{9,10},{10,1... | collective-permute-start | bytes 786440 | tf_op jit(solution)/shard_map/ppermute | solution.py:527
  212.2 0.7 broadcast_in_dim_reshape.3.refs_7_.refs_8_
  212.9 7.8 %collective-permute-start.34 = (bf16[256,512]{1,0:T(8,128)(2,1)}, bf16[256,512]{1,0:T(8,128)(2,1)S(1)}, u32[]{:S(2)}, u32[]{:S(2)}) collective-permute-start(bf16[256,512]{1,0:T(8,128)(2,1)} %get-tuple-element.113), channel_id=1, source_target_pairs={{0,2},{1,3},{2,4},{3,5},{4,6},{5,7},{6,0},{7,1},{8,10},{9,11},{10,... | collective-permute-start | bytes 786440 | tf_op jit(solution)/shard_map/ppermute | solution.py:527
  220.7 1.8 collective-permute-start.35
  222.5 2.6 collective-permute-start.36
  225.1 3.4 %collective-permute-start.37 = (bf16[256,512]{1,0:T(8,128)(2,1)}, bf16[256,512]{1,0:T(8,128)(2,1)}, u32[]{:S(2)}, u32[]{:S(2)}) collective-permute-start(bf16[256,512]{1,0:T(8,128)(2,1)} %get-tuple-element.116), channel_id=1, source_target_pairs={{0,5},{1,6},{2,7},{3,0},{4,1},{5,2},{6,3},{7,4},{8,13},{9,14},{10,... | collective-permute-start | bytes 786440 | tf_op jit(solution)/shard_map/ppermute | solution.py:527
  228.4 6.0 %emit.4 = (bf16[2048,2048]{1,0:T(8,128)(2,1)}, f32[8,128]{1,0:T(8,128)}) custom-call(bf16[2048,512]{1,0:T(8,128)(2,1)} %get-tuple-element.84.refs_0_, bf16[2048,512]{1,0:T(8,128)(2,1)} %get-tuple-element.85.refs_1_, bf16[2048,512]{1,0:T(8,128)(2,1)} %get-tuple-element.86.refs_2_, bf16[2048,256]{1,0:T(8,128)(2,1)} %get-tuple-element.87.refs_3_.refs_4_, ...), custom_call_target="tpu_custom_call" | custom-call | flops 1610612736 | bytes 11534336 | tf_op jit(solution)/shard_map/emit/pallas_call | solution.py:470
  234.4 9.3 %convolve.5 = (bf16[2048,512]{1,0:T(8,128)(2,1)}, bf16[2048,512]{1,0:T(8,128)(2,1)}, bf16[2048,512]{1,0:T(8,128)(2,1)}, bf16[256,512]{1,0:T(8,128)(2,1)}) custom-call(s32[1]{0:T(128)} %bitcast.me_ref, bf16[256,16384]{1,0:T(8,128)(2,1)} %x_ref.11, bf16[256,512]{1,0:T(8,128)(2,1)} %collective-permute-done.20.refs_0_, ...), custom_call_target="tpu_custom_call" | custom-call | flops 536870912 | bytes 8388608 | tf_op jit(solution)/shard_map/convolve/pallas_call | solution.py:383
  243.7 1.3 collective-permute-start.27
  245.0 2.0 collective-permute-start.28
  247.0 3.3 %collective-permute-done.35.refs_2_ = bf16[256,512]{1,0:T(8,128)(2,1)} collective-permute-done((bf16[256,512]{1,0:T(8,128)(2,1)}, bf16[256,512]{1,0:T(8,128)(2,1)}, u32[]{:S(2)}, u32[]{:S(2)}) %collective-permute-start.35) | collective-permute-done | bytes 262176 | tf_op jit(solution)/shard_map/ppermute | solution.py:527
  250.3 2.0 collective-permute-start.29
  252.3 6.8 %collective-permute-start.38 = (bf16[256,512]{1,0:T(8,128)(2,1)}, bf16[256,512]{1,0:T(8,128)(2,1)}, u32[]{:S(2)}, u32[]{:S(2)}) collective-permute-start(bf16[256,512]{1,0:T(8,128)(2,1)} %get-tuple-element.117), channel_id=1, source_target_pairs={{0,6},{1,7},{2,0},{3,1},{4,2},{5,3},{6,4},{7,5},{8,14},{9,15},{10,... | collective-permute-start | bytes 786440 | tf_op jit(solution)/shard_map/ppermute | solution.py:527
  259.1 1.5 collective-permute-start.39
  260.6 9.2 %convolve.6 = (bf16[2048,512]{1,0:T(8,128)(2,1)}, bf16[2048,512]{1,0:T(8,128)(2,1)}, bf16[2048,512]{1,0:T(8,128)(2,1)}, bf16[256,512]{1,0:T(8,128)(2,1)}) custom-call(s32[1]{0:T(128)} %bitcast.me_ref, bf16[256,16384]{1,0:T(8,128)(2,1)} %x_ref.11, bf16[8,256,512]{2,1,0:T(8,128)(2,1)} %all-to-all-done.1.refs_0_, bf16[4,2560]{1,0:T(4,128)(2,1)} %copy-done.2, ...), custom_call_target="tpu_custom_call" | custom-call | flops 536870912 | bytes 8388608 | tf_op jit(solution)/shard_map/convolve/pallas_call | solution.py:383
  269.8 1.3 collective-permute-start.30
  271.2 1.3 collective-permute-start.31
  272.5 2.0 collective-permute-start.32
  274.5 6.0 %emit.5 = (bf16[2048,2048]{1,0:T(8,128)(2,1)}, f32[8,128]{1,0:T(8,128)}) custom-call(bf16[2048,2048]{1,0:T(8,128)(2,1)} %get-tuple-element.92.refs_0_, bf16[2048,512]{1,0:T(8,128)(2,1)} %get-tuple-element.101.refs_1_, bf16[2048,512]{1,0:T(8,128)(2,1)} %get-tuple-element.102.refs_2_, ...), custom_call_target="tpu_custom_call", output_to_operand_aliasing={{0}: (0, {})} | custom-call | flops 1610612736 | bytes 11534336 | tf_op jit(solution)/shard_map/emit/pallas_call | solution.py:470
  280.5 9.3 %convolve.7 = (bf16[2048,512]{1,0:T(8,128)(2,1)}, bf16[2048,512]{1,0:T(8,128)(2,1)}, bf16[2048,512]{1,0:T(8,128)(2,1)}, bf16[256,512]{1,0:T(8,128)(2,1)}) custom-call(s32[1]{0:T(128)} %bitcast.me_ref, bf16[256,16384]{1,0:T(8,128)(2,1)} %x_ref.11, bf16[256,512]{1,0:T(8,128)(2,1)} %copy-done.9, bf16[256,512]{1,0:T(8,128)(2,1)} %copy-done.10, ...), custom_call_target="tpu_custom_call" | custom-call | flops 536870912 | bytes 8388608 | tf_op jit(solution)/shard_map/convolve/pallas_call | solution.py:383
  289.8 1.3 collective-permute-start.40
  291.1 2.0 collective-permute-start.41
  293.1 2.0 collective-permute-start.42
  295.1 0.7 copy-done.4
  295.8 6.0 %emit.6 = (bf16[2048,2048]{1,0:T(8,128)(2,1)}, f32[8,128]{1,0:T(8,128)}) custom-call(bf16[2048,2048]{1,0:T(8,128)(2,1)} %get-tuple-element.105.refs_0_, bf16[2048,512]{1,0:T(8,128)(2,1)} %get-tuple-element.107.refs_1_, bf16[2048,512]{1,0:T(8,128)(2,1)} %get-tuple-element.108.refs_2_, ...), custom_call_target="tpu_custom_call", output_to_operand_aliasing={{0}: (0, {})} | custom-call | flops 1610612736 | bytes 11534336 | tf_op jit(solution)/shard_map/emit/pallas_call | solution.py:470
  301.8 0.7 copy-done.6
  302.5 6.0 %emit.7 = (bf16[2048,2048]{1,0:T(8,128)(2,1)}, f32[8,128]{1,0:T(8,128)}) custom-call(bf16[2048,2048]{1,0:T(8,128)(2,1)} %get-tuple-element.111.refs_0_, bf16[2048,512]{1,0:T(8,128)(2,1)} %get-tuple-element.120.refs_1_, bf16[2048,512]{1,0:T(8,128)(2,1)} %get-tuple-element.121.refs_2_, ...), custom_call_target="tpu_custom_call", output_to_operand_aliasing={{0}: (0, {})} | custom-call | flops 1610612736 | bytes 11534336 | tf_op jit(solution)/shard_map/emit/pallas_call | solution.py:470
  (82 shorter events, 1.8 us)
Async XLA Ops:
  0.0 178.6 %copy-start = (f32[4,16384]{1,0:T(4,128)S(1)}, f32[4,16384]{1,0:T(4,128)}, u32[]{:S(2)}) copy-start(f32[4,16384]{1,0:T(4,128)} %param.16) | copy-start | bytes 786436
  3.2 58.4 %all-to-all-start = ((bf16[8,272,512]{2,1,0:T(8,128)(2,1)}), bf16[8,272,512]{2,1,0:T(8,128)(2,1)}, u32[]{:S(2)}, u32[]{:S(2)}) async-start(bf16[8,272,512]{2,1,0:T(8,128)(2,1)} %pack_bc.1), calls=%async_computation | async-start | bytes 4456448 | tf_op jit(solution)/shard_map/all_to_all | solution.py:538
  61.6 198.9 %all-to-all-start.1 = ((bf16[8,256,512]{2,1,0:T(8,128)(2,1)}), bf16[8,256,512]{2,1,0:T(8,128)(2,1)}, u32[]{:S(2)}, u32[]{:S(2)}) async-start(bf16[8,256,512]{2,1,0:T(8,128)(2,1)} %get-tuple-element.106), calls=%async_computation.1 | async-start | bytes 4194304 | tf_op jit(solution)/shard_map/all_to_all | solution.py:538
  66.0 45.8 %collective-permute-start = (bf16[256,512]{1,0:T(8,128)(2,1)}, bf16[256,512]{1,0:T(8,128)(2,1)S(1)}, u32[]{:S(2)}, u32[]{:S(2)}) collective-permute-start(bf16[256,512]{1,0:T(8,128)(2,1)} %get-tuple-element.65), channel_id=1, source_target_pairs={{0,1},{1,2},{2,3},{3,4},{4,5},{5,6},{6,7},{7,0},{8,9},{9,10},{10,1... | collective-permute-start | bytes 786440 | tf_op jit(solution)/shard_map/ppermute | solution.py:527
  67.9 63.5 %collective-permute-start.1 = (bf16[256,512]{1,0:T(8,128)(2,1)}, bf16[256,512]{1,0:T(8,128)(2,1)S(1)}, u32[]{:S(2)}, u32[]{:S(2)}) collective-permute-start(bf16[256,512]{1,0:T(8,128)(2,1)} %get-tuple-element.66), channel_id=1, source_target_pairs={{0,2},{1,3},{2,4},{3,5},{4,6},{5,7},{6,0},{7,1},{8,10},{9,11},{10,... | collective-permute-start | bytes 786440 | tf_op jit(solution)/shard_map/ppermute | solution.py:527
  69.4 9.5 %copy-start.14 = (f32[256]{0:T(256)S(1)}, f32[256]{0:T(256)}, u32[]{:S(2)}) copy-start(f32[256]{0:T(256)} %param.14) | copy-start | bytes 3076
  69.4 9.5 %copy-start.15 = (f32[256]{0:T(256)S(1)}, f32[256]{0:T(256)}, u32[]{:S(2)}) copy-start(f32[256]{0:T(256)} %param.13) | copy-start | bytes 3076
  69.4 76.3 %collective-permute-start.2 = (bf16[256,512]{1,0:T(8,128)(2,1)}, bf16[256,512]{1,0:T(8,128)(2,1)}, u32[]{:S(2)}, u32[]{:S(2)}) collective-permute-start(bf16[256,512]{1,0:T(8,128)(2,1)} %get-tuple-element.67), channel_id=1, source_target_pairs={{0,3},{1,4},{2,5},{3,6},{4,7},{5,0},{6,1},{7,2},{8,11},{9,12},{10,... | collective-permute-start | bytes 786440 | tf_op jit(solution)/shard_map/ppermute | solution.py:527
  73.5 1.3 collective-permute-start.14
  74.1 1.4 collective-permute-start.13
  74.8 1.4 collective-permute-start.12
  75.5 1.4 collective-permute-start.11
  76.2 1.4 collective-permute-start.10
  76.8 1.4 collective-permute-start.9
  77.5 2.8 collective-permute-start.7
  78.2 3.6 %collective-permute-start.8 = (bf16[4,2560]{1,0:T(4,128)(2,1)}, bf16[4,2560]{1,0:T(4,128)(2,1)S(1)}, u32[]{:S(2)}, u32[]{:S(2)}) collective-permute-start(bf16[4,2560]{1,0:T(4,128)(2,1)} %get-tuple-element.73), channel_id=1, source_target_pairs={{7,9},{15,17},{23,25}} | collective-permute-start | bytes 61448 | tf_op jit(solution)/shard_map/ppermute | solution.py:551
  80.4 78.2 %collective-permute-start.3 = (bf16[256,512]{1,0:T(8,128)(2,1)}, bf16[256,512]{1,0:T(8,128)(2,1)}, u32[]{:S(2)}, u32[]{:S(2)}) collective-permute-start(bf16[256,512]{1,0:T(8,128)(2,1)} %get-tuple-element.68), channel_id=1, source_target_pairs={{0,4},{1,5},{2,6},{3,7},{4,0},{5,1},{6,2},{7,3},{8,12},{9,13},{10,... | collective-permute-start | bytes 786440 | tf_op jit(solution)/shard_map/ppermute | solution.py:527
  81.8 78.1 %collective-permute-start.4 = (bf16[256,512]{1,0:T(8,128)(2,1)}, bf16[256,512]{1,0:T(8,128)(2,1)}, u32[]{:S(2)}, u32[]{:S(2)}) collective-permute-start(bf16[256,512]{1,0:T(8,128)(2,1)} %get-tuple-element.69), channel_id=1, source_target_pairs={{0,5},{1,6},{2,7},{3,0},{4,1},{5,2},{6,3},{7,4},{8,13},{9,14},{10,... | collective-permute-start | bytes 786440 | tf_op jit(solution)/shard_map/ppermute | solution.py:527
  111.8 68.7 %copy-start.7 = (bf16[256,512]{1,0:T(8,128)(2,1)}, bf16[256,512]{1,0:T(8,128)(2,1)S(1)}, u32[]{:S(2)}) copy-start(bf16[256,512]{1,0:T(8,128)(2,1)S(1)} %collective-permute-done.refs_0_) | copy-start | bytes 786436
  111.8 51.2 %collective-permute-start.5 = (bf16[256,512]{1,0:T(8,128)(2,1)}, bf16[256,512]{1,0:T(8,128)(2,1)}, u32[]{:S(2)}, u32[]{:S(2)}) collective-permute-start(bf16[256,512]{1,0:T(8,128)(2,1)} %get-tuple-element.70), channel_id=1, source_target_pairs={{0,6},{1,7},{2,0},{3,1},{4,2},{5,3},{6,4},{7,5},{8,14},{9,15},{10,... | collective-permute-start | bytes 786440 | tf_op jit(solution)/shard_map/ppermute | solution.py:527
  131.4 49.1 %copy-start.8 = (bf16[256,512]{1,0:T(8,128)(2,1)}, bf16[256,512]{1,0:T(8,128)(2,1)S(1)}, u32[]{:S(2)}) copy-start(bf16[256,512]{1,0:T(8,128)(2,1)S(1)} %collective-permute-done.1.refs_1_) | copy-start | bytes 786436
  131.4 40.4 %collective-permute-start.6 = (bf16[256,512]{1,0:T(8,128)(2,1)}, bf16[256,512]{1,0:T(8,128)(2,1)}, u32[]{:S(2)}, u32[]{:S(2)}) collective-permute-start(bf16[256,512]{1,0:T(8,128)(2,1)} %get-tuple-element.71), channel_id=1, source_target_pairs={{0,7},{1,0},{2,1},{3,2},{4,3},{5,4},{6,5},{7,6},{8,15},{9,8},{10,9... | collective-permute-start | bytes 786440 | tf_op jit(solution)/shard_map/ppermute | solution.py:527
  145.7 30.4 %collective-permute-start.20 = (bf16[256,512]{1,0:T(8,128)(2,1)}, bf16[256,512]{1,0:T(8,128)(2,1)}, u32[]{:S(2)}, u32[]{:S(2)}) collective-permute-start(bf16[256,512]{1,0:T(8,128)(2,1)} %get-tuple-element.93), channel_id=1, source_target_pairs={{0,1},{1,2},{2,3},{3,4},{4,5},{5,6},{6,7},{7,0},{8,9},{9,10},{10,1... | collective-permute-start | bytes 786440 | tf_op jit(solution)/shard_map/ppermute | solution.py:527
  145.7 34.8 %copy-start.2 = (bf16[4,2560]{1,0:T(4,128)(2,1)}, bf16[4,2560]{1,0:T(4,128)(2,1)S(1)}, u32[]{:S(2)}) copy-start(bf16[4,2560]{1,0:T(4,128)(2,1)S(1)} %add_add_fusion.refs_7_.refs_1_) | copy-start | bytes 61444
  158.6 17.5 %collective-permute-start.15 = (f32[8,128]{1,0:T(8,128)}, f32[8,128]{1,0:T(8,128)S(1)}, u32[]{:S(2)}, u32[]{:S(2)}) collective-permute-start(f32[8,128]{1,0:T(8,128)} %get-tuple-element.83), channel_id=1, source_target_pairs={{0,8},{8,16},{16,24},{1,9},{9,17},{17,25},{2,10},{10,18},{18,26},{... | collective-permute-start | bytes 12296 | tf_op jit(solution)/shard_map/ppermute | solution.py:532
  159.9 18.6 %collective-permute-start.16 = (f32[8,128]{1,0:T(8,128)}, f32[8,128]{1,0:T(8,128)S(1)}, u32[]{:S(2)}, u32[]{:S(2)}) collective-permute-start(f32[8,128]{1,0:T(8,128)} %get-tuple-element.83), channel_id=1, source_target_pairs={{0,16},{8,24},{1,17},{9,25},{2,18},{10,26},{3,19},{11,27},{4,20},{... | collective-permute-start | bytes 12296 | tf_op jit(solution)/shard_map/ppermute | solution.py:532
  163.1 26.8 %collective-permute-start.21 = (bf16[256,512]{1,0:T(8,128)(2,1)}, bf16[256,512]{1,0:T(8,128)(2,1)}, u32[]{:S(2)}, u32[]{:S(2)}) collective-permute-start(bf16[256,512]{1,0:T(8,128)(2,1)} %get-tuple-element.94), channel_id=1, source_target_pairs={{0,2},{1,3},{2,4},{3,5},{4,6},{5,7},{6,0},{7,1},{8,10},{9,11},{10,... | collective-permute-start | bytes 786440 | tf_op jit(solution)/shard_map/ppermute | solution.py:527
  171.8 21.5 %collective-permute-start.22 = (bf16[256,512]{1,0:T(8,128)(2,1)}, bf16[256,512]{1,0:T(8,128)(2,1)}, u32[]{:S(2)}, u32[]{:S(2)}) collective-permute-start(bf16[256,512]{1,0:T(8,128)(2,1)} %get-tuple-element.95), channel_id=1, source_target_pairs={{0,3},{1,4},{2,5},{3,6},{4,7},{5,0},{6,1},{7,2},{8,11},{9,12},{10,... | collective-permute-start | bytes 786440 | tf_op jit(solution)/shard_map/ppermute | solution.py:527
  176.1 26.9 %collective-permute-start.23 = (bf16[256,512]{1,0:T(8,128)(2,1)}, bf16[256,512]{1,0:T(8,128)(2,1)}, u32[]{:S(2)}, u32[]{:S(2)}) collective-permute-start(bf16[256,512]{1,0:T(8,128)(2,1)} %get-tuple-element.96), channel_id=1, source_target_pairs={{0,4},{1,5},{2,6},{3,7},{4,0},{5,1},{6,2},{7,3},{8,12},{9,13},{10,... | collective-permute-start | bytes 786440 | tf_op jit(solution)/shard_map/ppermute | solution.py:527
  176.1 4.4 %copy-start.12 = (f32[8,128]{1,0:T(8,128)}, f32[8,128]{1,0:T(8,128)S(1)}, u32[]{:S(2)}) copy-start(f32[8,128]{1,0:T(8,128)S(1)} %collective-permute-done.15.refs_13_.refs_11_.refs_12_) | copy-start | bytes 12292
  176.1 28.9 %collective-permute-start.24 = (bf16[256,512]{1,0:T(8,128)(2,1)}, bf16[256,512]{1,0:T(8,128)(2,1)}, u32[]{:S(2)}, u32[]{:S(2)}) collective-permute-start(bf16[256,512]{1,0:T(8,128)(2,1)} %get-tuple-element.97), channel_id=1, source_target_pairs={{0,5},{1,6},{2,7},{3,0},{4,1},{5,2},{6,3},{7,4},{8,13},{9,14},{10,... | collective-permute-start | bytes 786440 | tf_op jit(solution)/shard_map/ppermute | solution.py:527
  178.5 2.1 copy-start.13
  178.5 28.6 %collective-permute-start.25 = (bf16[256,512]{1,0:T(8,128)(2,1)}, bf16[256,512]{1,0:T(8,128)(2,1)}, u32[]{:S(2)}, u32[]{:S(2)}) collective-permute-start(bf16[256,512]{1,0:T(8,128)(2,1)} %get-tuple-element.98), channel_id=1, source_target_pairs={{0,6},{1,7},{2,0},{3,1},{4,2},{5,3},{6,4},{7,5},{8,14},{9,15},{10,... | collective-permute-start | bytes 786440 | tf_op jit(solution)/shard_map/ppermute | solution.py:527
  180.6 31.5 %copy-start.16 = (f32[256]{0:T(256)S(1)}, f32[256]{0:T(256)}, u32[]{:S(2)}) copy-start(f32[256]{0:T(256)} %param.15) | copy-start | bytes 3076
  189.9 23.0 %collective-permute-start.26 = (bf16[256,512]{1,0:T(8,128)(2,1)}, bf16[256,512]{1,0:T(8,128)(2,1)S(1)}, u32[]{:S(2)}, u32[]{:S(2)}) collective-permute-start(bf16[256,512]{1,0:T(8,128)(2,1)} %get-tuple-element.99), channel_id=1, source_target_pairs={{0,7},{1,0},{2,1},{3,2},{4,3},{5,4},{6,5},{7,6},{8,15},{9,8},{10,9... | collective-permute-start | bytes 786440 | tf_op jit(solution)/shard_map/ppermute | solution.py:527
  193.3 27.4 %collective-permute-start.17 = (bf16[256,512]{1,0:T(8,128)(2,1)}, bf16[256,512]{1,0:T(8,128)(2,1)}, u32[]{:S(2)}, u32[]{:S(2)}) collective-permute-start(bf16[256,512]{1,0:T(8,128)(2,1)} %get-tuple-element.91), channel_id=1, source_target_pairs={{0,8},{8,16},{16,24},{1,9},{9,17},{17,25},{2,10},{10,18},{18,26},{... | collective-permute-start | bytes 786440 | tf_op jit(solution)/shard_map/ppermute | solution.py:532
  203.0 19.4 %collective-permute-start.18 = (bf16[256,512]{1,0:T(8,128)(2,1)}, bf16[256,512]{1,0:T(8,128)(2,1)}, u32[]{:S(2)}, u32[]{:S(2)}) collective-permute-start(bf16[256,512]{1,0:T(8,128)(2,1)} %get-tuple-element.91), channel_id=1, source_target_pairs={{0,16},{8,24},{1,17},{9,25},{2,18},{10,26},{3,19},{11,27},{4,20},{... | collective-permute-start | bytes 786440 | tf_op jit(solution)/shard_map/ppermute | solution.py:532
  205.0 20.0 %collective-permute-start.19 = (bf16[256,512]{1,0:T(8,128)(2,1)}, bf16[256,512]{1,0:T(8,128)(2,1)}, u32[]{:S(2)}, u32[]{:S(2)}) collective-permute-start(bf16[256,512]{1,0:T(8,128)(2,1)} %get-tuple-element.91), channel_id=1, source_target_pairs={{0,24},{1,25},{2,26},{3,27},{4,28},{5,29},{6,30},{7,31}} | collective-permute-start | bytes 786440 | tf_op jit(solution)/shard_map/ppermute | solution.py:532
  207.0 36.7 %collective-permute-start.33 = (bf16[256,512]{1,0:T(8,128)(2,1)}, bf16[256,512]{1,0:T(8,128)(2,1)S(1)}, u32[]{:S(2)}, u32[]{:S(2)}) collective-permute-start(bf16[256,512]{1,0:T(8,128)(2,1)} %get-tuple-element.112), channel_id=1, source_target_pairs={{0,1},{1,2},{2,3},{3,4},{4,5},{5,6},{6,7},{7,0},{8,9},{9,10},{10,1... | collective-permute-start | bytes 786440 | tf_op jit(solution)/shard_map/ppermute | solution.py:527
  212.9 21.5 %copy-start.11 = (bf16[256,512]{1,0:T(8,128)(2,1)}, bf16[256,512]{1,0:T(8,128)(2,1)S(1)}, u32[]{:S(2)}) copy-start(bf16[256,512]{1,0:T(8,128)(2,1)S(1)} %collective-permute-done.26.refs_6_) | copy-start | bytes 786436
  212.9 32.2 %collective-permute-start.34 = (bf16[256,512]{1,0:T(8,128)(2,1)}, bf16[256,512]{1,0:T(8,128)(2,1)S(1)}, u32[]{:S(2)}, u32[]{:S(2)}) collective-permute-start(bf16[256,512]{1,0:T(8,128)(2,1)} %get-tuple-element.113), channel_id=1, source_target_pairs={{0,2},{1,3},{2,4},{3,5},{4,6},{5,7},{6,0},{7,1},{8,10},{9,11},{10,... | collective-permute-start | bytes 786440 | tf_op jit(solution)/shard_map/ppermute | solution.py:527
  220.7 29.6 %collective-permute-start.35 = (bf16[256,512]{1,0:T(8,128)(2,1)}, bf16[256,512]{1,0:T(8,128)(2,1)}, u32[]{:S(2)}, u32[]{:S(2)}) collective-permute-start(bf16[256,512]{1,0:T(8,128)(2,1)} %get-tuple-element.114), channel_id=1, source_target_pairs={{0,3},{1,4},{2,5},{3,6},{4,7},{5,0},{6,1},{7,2},{8,11},{9,12},{10,... | collective-permute-start | bytes 786440 | tf_op jit(solution)/shard_map/ppermute | solution.py:527
  222.5 29.8 %collective-permute-start.36 = (bf16[256,512]{1,0:T(8,128)(2,1)}, bf16[256,512]{1,0:T(8,128)(2,1)}, u32[]{:S(2)}, u32[]{:S(2)}) collective-permute-start(bf16[256,512]{1,0:T(8,128)(2,1)} %get-tuple-element.115), channel_id=1, source_target_pairs={{0,4},{1,5},{2,6},{3,7},{4,0},{5,1},{6,2},{7,3},{8,12},{9,13},{10,... | collective-permute-start | bytes 786440 | tf_op jit(solution)/shard_map/ppermute | solution.py:527
  225.1 34.0 %collective-permute-start.37 = (bf16[256,512]{1,0:T(8,128)(2,1)}, bf16[256,512]{1,0:T(8,128)(2,1)}, u32[]{:S(2)}, u32[]{:S(2)}) collective-permute-start(bf16[256,512]{1,0:T(8,128)(2,1)} %get-tuple-element.116), channel_id=1, source_target_pairs={{0,5},{1,6},{2,7},{3,0},{4,1},{5,2},{6,3},{7,4},{8,13},{9,14},{10,... | collective-permute-start | bytes 786440 | tf_op jit(solution)/shard_map/ppermute | solution.py:527
  243.7 26.1 %copy-start.9 = (bf16[256,512]{1,0:T(8,128)(2,1)}, bf16[256,512]{1,0:T(8,128)(2,1)S(1)}, u32[]{:S(2)}) copy-start(bf16[256,512]{1,0:T(8,128)(2,1)S(1)} %collective-permute-done.33.refs_0_) | copy-start | bytes 786436
  243.7 26.1 %collective-permute-start.27 = (bf16[256,512]{1,0:T(8,128)(2,1)}, bf16[256,512]{1,0:T(8,128)(2,1)S(1)}, u32[]{:S(2)}, u32[]{:S(2)}) collective-permute-start(bf16[256,512]{1,0:T(8,128)(2,1)} %get-tuple-element.104), channel_id=1, source_target_pairs={{0,8},{8,16},{16,24},{1,9},{9,17},{17,25},{2,10},{10,18},{18,26},{... | collective-permute-start | bytes 786440 | tf_op jit(solution)/shard_map/ppermute | solution.py:532
  245.0 24.8 %copy-start.10 = (bf16[256,512]{1,0:T(8,128)(2,1)}, bf16[256,512]{1,0:T(8,128)(2,1)S(1)}, u32[]{:S(2)}) copy-start(bf16[256,512]{1,0:T(8,128)(2,1)S(1)} %collective-permute-done.34.refs_1_) | copy-start | bytes 786436
  245.0 26.1 %collective-permute-start.28 = (bf16[256,512]{1,0:T(8,128)(2,1)}, bf16[256,512]{1,0:T(8,128)(2,1)}, u32[]{:S(2)}, u32[]{:S(2)}) collective-permute-start(bf16[256,512]{1,0:T(8,128)(2,1)} %get-tuple-element.104), channel_id=1, source_target_pairs={{0,16},{8,24},{1,17},{9,25},{2,18},{10,26},{3,19},{11,27},{4,20},{... | collective-permute-start | bytes 786440 | tf_op jit(solution)/shard_map/ppermute | solution.py:532
  250.3 22.2 %collective-permute-start.29 = (bf16[256,512]{1,0:T(8,128)(2,1)}, bf16[256,512]{1,0:T(8,128)(2,1)}, u32[]{:S(2)}, u32[]{:S(2)}) collective-permute-start(bf16[256,512]{1,0:T(8,128)(2,1)} %get-tuple-element.104), channel_id=1, source_target_pairs={{0,24},{1,25},{2,26},{3,27},{4,28},{5,29},{6,30},{7,31}} | collective-permute-start | bytes 786440 | tf_op jit(solution)/shard_map/ppermute | solution.py:532
  252.3 28.2 %collective-permute-start.38 = (bf16[256,512]{1,0:T(8,128)(2,1)}, bf16[256,512]{1,0:T(8,128)(2,1)}, u32[]{:S(2)}, u32[]{:S(2)}) collective-permute-start(bf16[256,512]{1,0:T(8,128)(2,1)} %get-tuple-element.117), channel_id=1, source_target_pairs={{0,6},{1,7},{2,0},{3,1},{4,2},{5,3},{6,4},{7,5},{8,14},{9,15},{10,... | collective-permute-start | bytes 786440 | tf_op jit(solution)/shard_map/ppermute | solution.py:527
  259.1 21.4 %collective-permute-start.39 = (bf16[256,512]{1,0:T(8,128)(2,1)}, bf16[256,512]{1,0:T(8,128)(2,1)}, u32[]{:S(2)}, u32[]{:S(2)}) collective-permute-start(bf16[256,512]{1,0:T(8,128)(2,1)} %get-tuple-element.118), channel_id=1, source_target_pairs={{0,7},{1,0},{2,1},{3,2},{4,3},{5,4},{6,5},{7,6},{8,15},{9,8},{10,9... | collective-permute-start | bytes 786440 | tf_op jit(solution)/shard_map/ppermute | solution.py:527
  269.8 4.7 %copy-start.5 = (bf16[256,512]{1,0:T(8,128)(2,1)}, bf16[256,512]{1,0:T(8,128)(2,1)S(1)}, u32[]{:S(2)}) copy-start(bf16[256,512]{1,0:T(8,128)(2,1)S(1)} %collective-permute-done.27.refs_9_) | copy-start | bytes 786436
  269.8 23.2 %collective-permute-start.30 = (bf16[256,512]{1,0:T(8,128)(2,1)}, bf16[256,512]{1,0:T(8,128)(2,1)S(1)}, u32[]{:S(2)}, u32[]{:S(2)}) collective-permute-start(bf16[256,512]{1,0:T(8,128)(2,1)} %get-tuple-element.110), channel_id=1, source_target_pairs={{0,8},{8,16},{16,24},{1,9},{9,17},{17,25},{2,10},{10,18},{18,26},{... | collective-permute-start | bytes 786440 | tf_op jit(solution)/shard_map/ppermute | solution.py:532
  271.2 23.9 %collective-permute-start.31 = (bf16[256,512]{1,0:T(8,128)(2,1)}, bf16[256,512]{1,0:T(8,128)(2,1)S(1)}, u32[]{:S(2)}, u32[]{:S(2)}) collective-permute-start(bf16[256,512]{1,0:T(8,128)(2,1)} %get-tuple-element.110), channel_id=1, source_target_pairs={{0,16},{8,24},{1,17},{9,25},{2,18},{10,26},{3,19},{11,27},{4,20},{... | collective-permute-start | bytes 786440 | tf_op jit(solution)/shard_map/ppermute | solution.py:532
  272.5 22.6 %collective-permute-start.32 = (bf16[256,512]{1,0:T(8,128)(2,1)}, bf16[256,512]{1,0:T(8,128)(2,1)}, u32[]{:S(2)}, u32[]{:S(2)}) collective-permute-start(bf16[256,512]{1,0:T(8,128)(2,1)} %get-tuple-element.110), channel_id=1, source_target_pairs={{0,24},{1,25},{2,26},{3,27},{4,28},{5,29},{6,30},{7,31}} | collective-permute-start | bytes 786440 | tf_op jit(solution)/shard_map/ppermute | solution.py:532
  289.8 12.0 %collective-permute-start.40 = (bf16[256,512]{1,0:T(8,128)(2,1)}, bf16[256,512]{1,0:T(8,128)(2,1)S(1)}, u32[]{:S(2)}, u32[]{:S(2)}) collective-permute-start(bf16[256,512]{1,0:T(8,128)(2,1)} %get-tuple-element.123), channel_id=1, source_target_pairs={{0,8},{8,16},{16,24},{1,9},{9,17},{17,25},{2,10},{10,18},{18,26},{... | collective-permute-start | bytes 786440 | tf_op jit(solution)/shard_map/ppermute | solution.py:532
  291.1 10.7 %collective-permute-start.41 = (bf16[256,512]{1,0:T(8,128)(2,1)}, bf16[256,512]{1,0:T(8,128)(2,1)}, u32[]{:S(2)}, u32[]{:S(2)}) collective-permute-start(bf16[256,512]{1,0:T(8,128)(2,1)} %get-tuple-element.123), channel_id=1, source_target_pairs={{0,16},{8,24},{1,17},{9,25},{2,18},{10,26},{3,19},{11,27},{4,20},{... | collective-permute-start | bytes 786440 | tf_op jit(solution)/shard_map/ppermute | solution.py:532
  293.1 2.0 copy-start.3
  293.1 8.7 %collective-permute-start.42 = (bf16[256,512]{1,0:T(8,128)(2,1)}, bf16[256,512]{1,0:T(8,128)(2,1)}, u32[]{:S(2)}, u32[]{:S(2)}) collective-permute-start(bf16[256,512]{1,0:T(8,128)(2,1)} %get-tuple-element.123), channel_id=1, source_target_pairs={{0,24},{1,25},{2,26},{3,27},{4,28},{5,29},{6,30},{7,31}} | collective-permute-start | bytes 786440 | tf_op jit(solution)/shard_map/ppermute | solution.py:532
  295.1 0.7 copy-start.4
  301.8 0.7 copy-start.6
  302.5 6.0 %copy-start.1 = (f32[4,16384]{1,0:T(4,128)S(1)}, f32[4,16384]{1,0:T(4,128)}, u32[]{:S(2)}) copy-start(f32[4,16384]{1,0:T(4,128)} %param.16) | copy-start | bytes 786436
